TPU v7x, 256 devices: a whole 4x4x8 slice. The times are simulated.
256 devices in a mesh: samp: 32 (over z, x), var: 8 (over y, core).
Axes of the slice: x: 4, y: 4, z: 8, core: 2. Of those that a mesh axis runs over, the one named last changes fastest.
Arguments:
- genotypes: bfloat16 [65536, 24576], P('samp', 'var'), as said below
- residuals: bfloat16 [65536, 4], P('samp')
- weights: bfloat16 [65536, 4], P('samp'), may hold values from 0.049804688 to 0.25
- block_regions: int32 [192], P('var'), may hold values from 0 to 1
- leads: int32 [16, 64], replicated, may hold values from 0 to 24575, as said below
Outputs:
- scores: float32 [4, 24576], P(None, 'var')
- variances: float32 [4, 24576], P(None, 'var')
Inputs may be any that keep to these rules, and one draw needn't show every extreme that they name: `block_regions`: each index of var owns 2 regions; a block names one of the regions owned by the var index that holds it. The 128 leads of the regions of one var index are distinct; at most 32 of them lie among the variants of any one var index, and exactly 32 lie on some var index. `genotypes`: dosages and weights are such that every gram is positive definite.
All inputs are finite; a program needn't handle non-finite values.
Results may differ from a plain program's by a relative error of at most 0.002.
Values may be sent and summed in bfloat16 or wider, within the bound.
A program may use at most 128 MiB of HBM per device.

v0:
```python
import math

import jax
import jax.numpy as jnp
from jax import lax
from jax.sharding import PartitionSpec as P

VB = 128
HOST = 32


def conditional(cross, score, diag, var_region, chol, lead_solved, total):
    count = cross.shape[0]
    traits = score.shape[1]
    nlead = lead_solved.shape[2]
    crossed = jnp.transpose(cross.reshape(count, traits, nlead), (1, 2, 0))
    tstat = jnp.zeros((traits, count), jnp.float32)
    varv = jnp.zeros((traits, count), jnp.float32)
    for region in range(chol.shape[0]):
        solved = jax.scipy.linalg.solve_triangular(chol[region], crossed, lower=True)
        t_region = score.T - jnp.einsum(
            "klj,kl->kj", solved, lead_solved[region], precision=lax.Precision.HIGHEST
        )
        v_region = diag.T - jnp.sum(solved * solved, axis=1)
        selected = var_region[None, :] == region
        tstat = jnp.where(selected, t_region, tstat)
        varv = jnp.where(selected, v_region, varv)
    return (tstat / math.sqrt(total), varv / total)


def body(genotypes, residuals, weights, block_regions, leads):
    samples, local_vars = genotypes.shape
    nvar = lax.axis_size("var")
    nsamp = lax.axis_size("samp")
    myself = lax.axis_index("var")
    regions_dev = leads.shape[0] // nvar
    nlead = leads.shape[1]
    traits = residuals.shape[1]
    slots_all = regions_dev * nlead
    listed = leads.reshape(nvar, slots_all)
    source = listed // local_vars
    offset = listed % local_vars
    hosted = source == myself
    ranked = jnp.cumsum(hosted.astype(jnp.int32), axis=1) - 1
    target = jnp.where(hosted, ranked, HOST)
    dest_rows = jnp.broadcast_to(jnp.arange(nvar, dtype=jnp.int32)[:, None], (nvar, slots_all))
    picked = jnp.zeros((nvar, HOST), jnp.int32).at[dest_rows, target].set(offset, mode="drop")
    outgoing = jnp.take(genotypes, picked.reshape(-1), axis=1)
    incoming = lax.all_to_all(outgoing, "var", split_axis=1, concat_axis=1, tiled=True)
    my_source = lax.dynamic_index_in_dim(source, myself, 0, keepdims=False)
    onehot = (my_source[:, None] == jnp.arange(nvar, dtype=jnp.int32)[None, :]).astype(jnp.int32)
    rank_in = jnp.sum((jnp.cumsum(onehot, axis=0) - 1) * onehot, axis=1)
    lead_cols = jnp.take(incoming, my_source * HOST + rank_in, axis=1).reshape(
        samples, regions_dev, nlead
    )
    weighted = (
        lead_cols[:, :, None, :].astype(jnp.float32) * weights[:, None, :, None].astype(jnp.float32)
    ).astype(jnp.bfloat16)
    gram = jnp.einsum("srkl,srm->rklm", weighted, lead_cols, preferred_element_type=jnp.float32)
    lead_score = jnp.einsum("srl,sk->rkl", lead_cols, residuals, preferred_element_type=jnp.float32)
    gram, lead_score = lax.psum((gram, lead_score), "samp")
    chol = jnp.linalg.cholesky(gram)
    lead_solved = jax.scipy.linalg.solve_triangular(chol, lead_score[..., None], lower=True)[..., 0]
    flat_weighted = weighted.reshape(samples, regions_dev * traits * nlead)
    columns_each = traits * nlead
    nblocks = local_vars // VB

    def block_cross(inputs):
        block, region = inputs
        block_cols = lax.dynamic_slice_in_dim(genotypes, block * VB, VB, 1)
        chosen = lax.dynamic_slice_in_dim(flat_weighted, region * columns_each, columns_each, 1)
        return lax.dot_general(
            block_cols, chosen, (((0,), (0,)), ((), ())), preferred_element_type=jnp.float32
        )

    cross = lax.map(block_cross, (jnp.arange(nblocks, dtype=jnp.int32), block_regions)).reshape(
        local_vars, columns_each
    )
    score = lax.dot_general(
        genotypes, residuals, (((0,), (0,)), ((), ())), preferred_element_type=jnp.float32
    )
    squared = genotypes * genotypes
    diag = lax.dot_general(
        squared, weights, (((0,), (0,)), ((), ())), preferred_element_type=jnp.float32
    )
    var_region = jnp.repeat(block_regions, VB)
    total = samples * nsamp
    cross, score, diag = lax.psum((cross, score, diag), "samp")
    scores, variances = conditional(cross, score, diag, var_region, chol, lead_solved, total)
    return (scores, variances)


def solution(mesh):
    in_specs = (P("samp", "var"), P("samp", None), P("samp", None), P("var"), P())
    out_specs = (P(None, "var"), P(None, "var"))
    return jax.shard_map(body, mesh=mesh, in_specs=in_specs, out_specs=out_specs, check_vma=False)
```

profile of v0, /device:TPU:32, one launch (start us, length us, event | category | flops | bytes accessed | tf_op | source)
XLA Modules:
  0.0 666.8 jit_solution(4114289144083290587)
XLA Ops:
  9.2 23.3 %fusion.40 = s32[8,128,1]{2,0,1:T(8,128)S(1)} fusion(s32[8,128,1]{2,0,1:T(8,128)S(1)} %copy.104), kind=kOutput, calls=%fused_computation.90 | output fusion | flops 130048 | bytes 8192 | tf_op jit(solution)/shard_map/jit(cumsum)/reduce_window_sum | solution.py:44
  34.6 4.3 scatter_custom_fusion
  39.0 16.7 %copy.113 = bf16[2048,3072]{0,1:T(8,128)(2,1)} copy(bf16[2048,3072]{1,0:T(8,128)(2,1)} %param.9) | data formatting | bytes 25165824 | tf_op args[0]
  55.7 8.6 %gather_fusion = bf16[256,2048]{1,0:T(8,128)(2,1)S(1)} fusion(bf16[2048,3072]{0,1:T(8,128)(2,1)} %copy.113, s32[1024]{0:T(1024)S(1)} %pad_clamp_fusion.1), kind=kCustom, calls=%fused_computation | custom fusion | bytes 2098176 | tf_op jit(solution)/shard_map/jit(_take)/gather | solution.py:48
  65.5 4.5 all-to-all-start
  71.3 14.6 %all-to-all-done = bf16[2048,8,32]{0,2,1:T(8,128)(2,1)S(1)} async-done(((bf16[2048,8,32]{0,2,1:T(8,128)(2,1)}), bf16[2048,8,32]{0,2,1:T(8,128)(2,1)S(1)}, u32[]{:S(2)}, u32[]{:S(2)}) %all-to-all-start) | async-done | bytes 1048608 | tf_op jit(solution)/shard_map/all_to_all | solution.py:49
  87.0 1.9 fusion.9
  89.2 208.0 %while.10 = (s32[]{:T(128)}, f32[24,128,256]{1,0,2:T(8,128)}, s32[24]{0:T(128)S(1)}, bf16[2048,3072]{1,0:T(8,128)(2,1)}, s32[24]{0:T(128)S(1)}, /*index=5*/bf16[...) while((s32[]{:T(128)}, f32[24,128,256]{1,0,2:T(8,128)}, ...), condition=%wide.region_9.10_spmd, body=%wide.region_8.9_spmd.sunk | while | flops 134217744 | bytes 1966325 | solution.py:76
  93.2 4.7 dynamic_update_slice.5
  101.9 4.7 dynamic_update_slice.5
  109.1 1.5 fusion.60
  110.6 4.7 dynamic_update_slice.5
  117.8 1.5 fusion.60
  119.3 4.7 dynamic_update_slice.5
  126.5 1.5 fusion.60
  128.0 4.7 dynamic_update_slice.5
  136.7 4.7 dynamic_update_slice.5
  143.9 1.5 fusion.60
  145.4 4.7 dynamic_update_slice.5
  152.6 1.5 fusion.60
  154.1 4.7 dynamic_update_slice.5
  161.3 1.5 fusion.60
  162.8 4.7 dynamic_update_slice.5
  169.9 1.5 fusion.60
  171.4 4.7 dynamic_update_slice.5
  178.6 1.5 fusion.60
  180.0 4.7 dynamic_update_slice.5
  187.2 1.5 fusion.60
  188.7 4.7 dynamic_update_slice.5
  195.9 1.5 fusion.60
  197.3 4.7 dynamic_update_slice.5
  204.5 1.5 fusion.60
  206.0 4.7 dynamic_update_slice.5
  213.1 1.5 fusion.60
  214.6 4.7 dynamic_update_slice.5
  221.8 1.5 fusion.60
  223.3 4.7 dynamic_update_slice.5
  230.4 1.5 fusion.60
  231.9 4.7 dynamic_update_slice.5
  240.6 4.7 dynamic_update_slice.5
  249.2 4.7 dynamic_update_slice.5
  257.9 4.7 dynamic_update_slice.5
  266.5 4.7 dynamic_update_slice.5
  273.7 1.5 fusion.60
  275.2 4.7 dynamic_update_slice.5
  282.4 1.5 fusion.60
  283.8 4.7 dynamic_update_slice.5
  291.0 1.5 fusion.60
  292.5 4.7 dynamic_update_slice.5
  297.2 4.5 reshape.273
  302.7 6.9 %fusion.41 = f32[4,3072]{1,0:T(4,128)} fusion(bf16[2048,4]{0,1:T(4,128)(2,1)S(1)} %copy-done, bf16[2048,3072]{1,0:T(8,128)(2,1)} %get-tuple-element.190), kind=kOutput, calls=%fused_computation.91 | convolution fusion | flops 50331648 | bytes 12648448 | tf_op jit(solution)/shard_map/dot_general | solution.py:79
  309.7 7.3 %fusion.6 = f32[4,3072]{1,0:T(4,128)} fusion(bf16[2048,4]{0,1:T(4,128)(2,1)S(1)} %copy-done.6, bf16[2048,3072]{1,0:T(8,128)(2,1)} %get-tuple-element.190), kind=kOutput, calls=%fused_computation.10 | convolution fusion | flops 56623104 | bytes 12648448 | tf_op jit(solution)/shard_map/dot_general | solution.py:83
  318.0 143.4 %all-reduce.7.cloned.1.call-done = (f32[4,64,3072]{2,1,0:T(8,128)}, f32[2,4,64,64]{2,3,1,0:T(8,128)}) async-done(((f32[4,64,3072]{2,1,0:T(8,128)}, f32[2,4,64,64]{2,3,1,0:T(8,128)}), (f32[4,64,3072]{2,1,0:T(8,128)}, f32[2,4,64,64]{2,3,1,0:T(8,128)})) %all-reduce.7.cloned.1.call-update) | async-done | bytes 3276816 | tf_op jit(solution)/shard_map/psum | solution.py:88
  462.6 1.7 fusion.14
  464.3 47.6 %custom-call.11 = f32[2,4,64,64]{3,2,1,0:T(8,128)S(1)} custom-call(f32[2,4,64,64]{3,2,1,0:T(8,128)} %fusion.14), custom_call_target="Cholesky" | custom-call | tf_op jit(solution)/shard_map/jit(cholesky)/cholesky | solution.py:62
  512.8 1.8 select_bitcast_fusion
  514.6 40.7 %custom-call.12 = f32[2,4,1,64,64]{3,4,2,1,0:T(8,128)} custom-call(f32[2,4,1,64,64]{4,3,2,1,0:T(8,128)} %get-tuple-element.85), custom_call_target="InvertDiagBlocksLowerTriangular" | custom-call | tf_op jit(solution)/shard_map/jit(_solve_triangular)/vmap(vmap())/triangular_solve | solution.py:63
  555.3 50.6 %all-reduce.5.cloned.1.call-done = (f32[4,3072]{1,0:T(4,128)}, f32[2,4,64]{2,1,0:T(4,128)}, f32[4,3072]{1,0:T(4,128)}) async-done(((f32[4,3072]{1,0:T(4,128)}, f32[2,4,64]{2,1,0:T(4,128)}, f32[4,3072]{1,0:T(4,128)}), (f32[4,3072]{1,0:T(4,128)}, f32[2,4,64]{2,1,0:T(4,128)}, f32[4,3072]{1,0:T(4,128)})) %all-reduce.5.cloned.1.call-update) | async-done | bytes 100368 | tf_op jit(solution)/shard_map/psum | solution.py:88
  609.1 20.4 %custom-call.14 = f32[4,1,64,64]{2,3,1,0:T(8,128)S(1)} custom-call(f32[4,1,64,64]{3,2,1,0:T(8,128)} %get-tuple-element.91), custom_call_target="InvertDiagBlocksLowerTriangular" | custom-call | tf_op jit(solution)/shard_map/jit(_solve_triangular)/vmap()/triangular_solve | solution.py:20
  629.5 19.9 %custom-call.15 = f32[4,1,64,64]{2,3,1,0:T(8,128)S(1)} custom-call(f32[4,1,64,64]{3,2,1,0:T(8,128)S(1)} %get-tuple-element.92), custom_call_target="InvertDiagBlocksLowerTriangular" | custom-call | tf_op jit(solution)/shard_map/jit(_solve_triangular)/vmap()/triangular_solve | solution.py:20
  649.4 3.1 multiply_reduce_fusion.1
  652.5 3.1 multiply_reduce_fusion
  655.7 1.8 fusion.42
  657.5 1.8 fusion.43
  (141 shorter events, 54.4 us)
Async XLA Ops:
  7.2 295.6 %copy-start = (bf16[2048,4]{0,1:T(4,128)(2,1)S(1)}, bf16[2048,4]{0,1:T(4,128)(2,1)}, u32[]{:S(2)}) copy-start(bf16[2048,4]{0,1:T(4,128)(2,1)} %param.10) | copy-start | bytes 49156
  64.3 6.9 %copy-start.6 = (bf16[2048,4]{0,1:T(4,128)(2,1)S(1)}, bf16[2048,4]{0,1:T(4,128)(2,1)}, u32[]{:S(2)}) copy-start(bf16[2048,4]{0,1:T(4,128)(2,1)} %param.11) | copy-start | bytes 49156
  65.5 20.4 %all-to-all-start = ((bf16[2048,8,32]{0,2,1:T(8,128)(2,1)}), bf16[2048,8,32]{0,2,1:T(8,128)(2,1)S(1)}, u32[]{:S(2)}, u32[]{:S(2)}) async-start(bf16[2048,8,32]{0,2,1:T(8,128)(2,1)} %broadcast_select_fusion), calls=%async_computation | async-start | bytes 2097152 | tf_op jit(solution)/shard_map/all_to_all | solution.py:49
  69.9 391.5 %all-reduce.7.cloned.1.call-start = ((), (), s32[]{:S(2)}) async-start(), calls=%async_computation.2 | async-start | bytes 6815744 | tf_op jit(solution)/shard_map/psum | solution.py:88
  87.0 2.3 copy-start.11
  301.8 304.1 %all-reduce.5.cloned.1.call-start = ((), (), s32[]{:S(2)}) async-start(), calls=%async_computation.1 | async-start | bytes 204800 | tf_op jit(solution)/shard_map/psum | solution.py:88
  302.0 210.8 %copy-start.3 = (pred[64,64]{1,0:T(8,128)(4,1)}, pred[64,64]{1,0:T(8,128)(4,1)S(1)}, u32[]{:S(2)}) copy-start(pred[64,64]{1,0:T(8,128)(4,1)S(1)} %iota_compare_fusion.1) | copy-start | bytes 12292
  461.4 188.0 %copy-start.1 = (f32[4,64,3072]{2,1,0:T(8,128)S(1)}, f32[4,64,3072]{2,1,0:T(8,128)}, u32[]{:S(2)}) copy-start(f32[4,64,3072]{2,1,0:T(8,128)} %get-tuple-element.83) | copy-start | bytes 9437188
  512.0 0.7 copy-start.2
  652.5 3.1 copy-start.10
  655.6 1.8 copy-start.9
  655.6 3.6 copy-start.4
  655.7 3.6 copy-start.5
  655.7 3.6 copy-start.7
  655.7 3.6 copy-start.8
Sparse Core Ops, SparseCore 0:
  301.9 159.4 all-reduce.6
  466.2 139.5 all-reduce.4
where the time goes:
time: 671 us; the launch traced here: 667 us
  waiting for transfers between devices  209 us (31%)
  local copies, waits for them, and re-layouts  181 us (27%)
  other arithmetic  163 us (24%)
  matrix products  63.3 us (9%)
  loops' own time  31.7 us (5%)
  between operations  14.4 us (2%)
    psum x2, waiting for transfers between devices, body(): cross, score, diag = lax.psum((cross, score, diag), 'samp')  194 us
    dynamic_update_slice x24, local copies, waits for them, and re-layouts, body(): lax.map(block_cross, (jnp.arange(nblocks, dtype=jnp.int32), block_regions))  113 us
    another operation x4, other arithmetic, body(): chol = jnp.linalg.cholesky(gram)  47.8 us
    another operation x2, other arithmetic, body(): jax.scipy.linalg.solve_triangular(chol, lead_score[..., None], lower=True)  42.5 us
    another operation x4, other arithmetic, conditional(): jax.scipy.linalg.solve_triangular(chol[region], crossed, lower=True)  41.6 us
    dot_general x24, matrix products, block_cross(): lax.dot_general(block_cols, chosen, (((0,), (0,)), ((), ())), preferred_e...  35.2 us
    another operation x1, loops' own time, body(): lax.map(block_cross, (jnp.arange(nblocks, dtype=jnp.int32), block_regions))  31.7 us
    dynamic_slice x48, local copies, waits for them, and re-layouts, body(): lax.map(block_cross, (jnp.arange(nblocks, dtype=jnp.int32), block_regions))  28.1 us
  transfers between devices with their start and end apart: 3, of which 3 were waited for; matrix products, arithmetic and copies ran while one was open for 17% of the time, Pallas kernels for 0%

commit v1 on v0

v1 whole, which is shorter than its diff:
```python
import functools
import math

import jax
import jax.numpy as jnp
from jax import lax
from jax.experimental import pallas as pl
from jax.experimental.pallas import tpu as pltpu
from jax.sharding import PartitionSpec as P

VB = 128
HOST = 32
NT = (((1,), (1,)), ((), ()))
NN = (((1,), (0,)), ((), ()))
EXTRA = 16


def gather_kernel(listed_ref, geno_ref, out_ref, onehot):
    nvar, slots = listed_ref.shape
    local_vars = geno_ref.shape[1]

    @pl.when(pl.program_id(0) == 0)
    def _():
        base = lax.axis_index("var") * local_vars
        offset = listed_ref[...] - base
        hosted = (offset >= 0) & (offset < local_vars)
        before = lax.broadcasted_iota(jnp.int32, (slots, slots), 0) < lax.broadcasted_iota(
            jnp.int32, (slots, slots), 1
        )
        rank = lax.dot_general(
            hosted.astype(jnp.float32),
            before.astype(jnp.float32),
            NN,
            preferred_element_type=jnp.float32,
        ).astype(jnp.int32)
        rank = jnp.where(hosted, rank, HOST)
        place = lax.broadcasted_iota(jnp.int32, (HOST, slots), 0)
        lanes = lax.broadcasted_iota(jnp.int32, (HOST, local_vars), 1)
        for owner in range(nvar):
            match = rank[owner : owner + 1, :] == place
            picked = jnp.sum(
                jnp.where(match, offset[owner : owner + 1, :], 0), axis=1, keepdims=True
            )
            onehot[owner * HOST : (owner + 1) * HOST, :] = (
                (lanes == picked).astype(jnp.float32).astype(jnp.bfloat16)
            )

    out_ref[...] = lax.dot_general(
        onehot[...], geno_ref[...], NT, preferred_element_type=jnp.float32
    ).astype(jnp.bfloat16)


def gather(listed, genotypes, tile=256):
    samples, local_vars = genotypes.shape
    nvar, slots = listed.shape
    rows = nvar * HOST
    return pl.pallas_call(
        gather_kernel,
        grid=(samples // tile,),
        in_specs=[
            pl.BlockSpec((nvar, slots), lambda i: (0, 0)),
            pl.BlockSpec((tile, local_vars), lambda i: (i, 0)),
        ],
        out_specs=pl.BlockSpec((rows, tile), lambda i: (0, i)),
        out_shape=jax.ShapeDtypeStruct((rows, samples), jnp.bfloat16),
        scratch_shapes=[pltpu.VMEM((rows, local_vars), jnp.bfloat16)],
        name="lead_gather",
    )(listed, genotypes)


def cross_kernel(region_ref, slot_ref, incoming_ref, side_ref, geno_ref, out_ref, lead, weighted, gram):
    nregion, rows, samples = weighted.shape
    nlead = lead.shape[0] // nregion
    traits = (rows - EXTRA) // nlead
    chunk = geno_ref.shape[1]
    step = pl.program_id(0)

    @pl.when(step == 0)
    def _():
        slots = incoming_ref.shape[0]
        pick = (
            lax.broadcasted_iota(jnp.int32, (nregion * nlead, slots), 1) == slot_ref[...]
        ).astype(jnp.float32).astype(jnp.bfloat16)
        lead[...] = lax.dot_general(
            pick, incoming_ref[...], NN, preferred_element_type=jnp.float32
        ).astype(jnp.bfloat16)
        for region in range(nregion):
            cols = lead[region * nlead : (region + 1) * nlead, :].astype(jnp.float32)
            for trait in range(traits):
                scale = side_ref[EXTRA + trait : EXTRA + trait + 1, :].astype(jnp.float32)
                weighted[region, trait * nlead : (trait + 1) * nlead, :] = (cols * scale).astype(
                    jnp.bfloat16
                )
            weighted[region, traits * nlead :, :] = side_ref[:EXTRA, :]
            gram[region] = lax.dot_general(
                weighted[region],
                lead[region * nlead : (region + 1) * nlead, :],
                NT,
                preferred_element_type=jnp.float32,
            )

    per_chunk = chunk // VB
    for block in range(per_chunk):
        region = region_ref[step * per_chunk + block]
        cols = geno_ref[:, block * VB : (block + 1) * VB]
        acc = lax.dot_general(weighted[region], cols, NN, preferred_element_type=jnp.float32)
        square = cols.astype(jnp.float32)
        square = (square * square).astype(jnp.bfloat16)
        diag = lax.dot_general(
            side_ref[EXTRA:, :], square, NN, preferred_element_type=jnp.float32
        )
        here = slice(block * VB, (block + 1) * VB)
        for trait in range(traits):
            out_ref[0, trait, :nlead, here] = acc[trait * nlead : (trait + 1) * nlead, :]
            out_ref[0, trait, nlead : nlead + 1, here] = acc[
                traits * nlead + trait : traits * nlead + trait + 1, :
            ]
            out_ref[0, trait, nlead + 1 : nlead + 2, here] = diag[trait : trait + 1, :]
            out_ref[0, trait, nlead + 2 :, here] = jnp.zeros((6, VB), jnp.float32)
    for trait in range(traits):
        out_ref[0, trait, nlead:, chunk:] = jnp.zeros((8, 2 * nlead), jnp.float32)
        for region in range(nregion):
            there = slice(chunk + region * nlead, chunk + (region + 1) * nlead)
            out_ref[0, trait, :nlead, there] = gram[region, trait * nlead : (trait + 1) * nlead, :]
            out_ref[0, trait, nlead : nlead + 1, there] = gram[
                region, traits * nlead + trait : traits * nlead + trait + 1, :
            ]


def cross_products(regions, slot, incoming, side, genotypes, traits, nregion, nchunk):
    samples, local_vars = genotypes.shape
    nlead = slot.shape[0] // nregion
    chunk = local_vars // nchunk
    rows = traits * nlead + EXTRA
    whole = lambda i, r: (0, 0)
    shape = (nchunk, traits, nlead + 8, chunk + nregion * nlead)
    return pl.pallas_call(
        cross_kernel,
        grid_spec=pltpu.PrefetchScalarGridSpec(
            num_scalar_prefetch=1,
            grid=(nchunk,),
            in_specs=[
                pl.BlockSpec(slot.shape, whole),
                pl.BlockSpec(incoming.shape, whole),
                pl.BlockSpec(side.shape, whole),
                pl.BlockSpec((samples, chunk), lambda i, r: (0, i)),
            ],
            out_specs=pl.BlockSpec((1,) + shape[1:], lambda i, r: (i, 0, 0, 0)),
            scratch_shapes=[
                pltpu.VMEM((nregion * nlead, samples), jnp.bfloat16),
                pltpu.VMEM((nregion, rows, samples), jnp.bfloat16),
                pltpu.VMEM((nregion, rows, nlead), jnp.float32),
            ],
        ),
        out_shape=jax.ShapeDtypeStruct(shape, jnp.float32),
        compiler_params=pltpu.CompilerParams(vmem_limit_bytes=48 * 1024 * 1024),
        name="cross_products",
    )(regions, slot, incoming, side, genotypes)


def finish_kernel(traits, total, region_ref, sum_ref, out_ref, inverse, pivots, target):
    nregion, nlead, _ = inverse.shape
    chunk = out_ref.shape[1]
    per_chunk = chunk // VB
    first = (lax.axis_index("samp") // traits) * per_chunk
    eye = (
        lax.broadcasted_iota(jnp.int32, (nlead, nlead), 0)
        == lax.broadcasted_iota(jnp.int32, (nlead, nlead), 1)
    )
    unit = eye.astype(jnp.float32)
    below = lax.broadcasted_iota(jnp.int32, (nlead, 1), 0)
    state = [
        jnp.concatenate(
            [sum_ref[:nlead, chunk + r * nlead : chunk + (r + 1) * nlead], unit], axis=1
        )
        for r in range(nregion)
    ]
    for j in range(nlead - 1):
        for r in range(nregion):
            row = state[r][j : j + 1, :]
            ratio = state[r][:, j : j + 1] / row[:, j : j + 1]
            state[r] = state[r] - jnp.where(below > j, ratio, 0.0) * row
    for r in range(nregion):
        lower = state[r][:, nlead:]
        upper = state[r][:, :nlead]
        inverse[r] = lower
        pivot = 1.0 / jnp.sum(jnp.where(eye, upper, 0.0), axis=1, keepdims=True)
        score = sum_ref[nlead : nlead + 1, chunk + r * nlead : chunk + (r + 1) * nlead]
        pivots[r] = jnp.broadcast_to(pivot, (nlead, VB))
        target[r] = jnp.broadcast_to(
            jnp.sum(lower * score, axis=1, keepdims=True) * pivot, (nlead, VB)
        )
    out_ref[...] = jnp.zeros_like(out_ref)
    for block in range(per_chunk):
        here = slice(block * VB, (block + 1) * VB)
        region = region_ref[first + block]
        solved = lax.dot_general(
            inverse[region],
            sum_ref[:nlead, here],
            NN,
            preferred_element_type=jnp.float32,
            precision=lax.Precision.HIGHEST,
        )
        fit = jnp.sum(solved * target[region], axis=0, keepdims=True)
        used = jnp.sum(solved * solved * pivots[region], axis=0, keepdims=True)
        out_ref[0:1, here] = (sum_ref[nlead : nlead + 1, here] - fit) / math.sqrt(total)
        out_ref[1:2, here] = (sum_ref[nlead + 1 : nlead + 2, here] - used) / total


def finish(regions, summed, traits, nlead, nregion, total):
    chunk = summed.shape[1] - nregion * nlead
    return pl.pallas_call(
        functools.partial(finish_kernel, traits, total),
        in_specs=[
            pl.BlockSpec(memory_space=pltpu.SMEM),
            pl.BlockSpec(memory_space=pltpu.VMEM),
        ],
        out_specs=pl.BlockSpec(memory_space=pltpu.VMEM),
        out_shape=jax.ShapeDtypeStruct((8, chunk), jnp.float32),
        scratch_shapes=[
            pltpu.VMEM((nregion, nlead, nlead), jnp.float32),
            pltpu.VMEM((nregion, nlead, VB), jnp.float32),
            pltpu.VMEM((nregion, nlead, VB), jnp.float32),
        ],
        name="conditional_finish",
    )(regions, summed)


def body(genotypes, residuals, weights, block_regions, leads):
    samples, local_vars = genotypes.shape
    nvar = lax.axis_size("var")
    nsamp = lax.axis_size("samp")
    myself = lax.axis_index("var")
    nregion = leads.shape[0] // nvar
    nlead = leads.shape[1]
    traits = residuals.shape[1]
    nchunk = nsamp // traits
    slots = nregion * nlead
    total = samples * nsamp
    listed = leads.reshape(nvar, slots)
    outgoing = gather(listed, genotypes)
    incoming = lax.all_to_all(outgoing, "var", split_axis=0, concat_axis=0, tiled=True)
    mine = lax.dynamic_index_in_dim(listed, myself, 0, keepdims=False)
    source = mine // local_vars
    order = jnp.arange(slots, dtype=jnp.int32)
    earlier = (source[:, None] == source[None, :]) & (order[None, :] < order[:, None])
    slot = source[:, None] * HOST + jnp.sum(earlier.astype(jnp.int32), axis=1, keepdims=True)
    pad = jnp.zeros((EXTRA - traits, samples), jnp.bfloat16)
    side = jnp.concatenate([residuals.T, pad, weights.T, pad], axis=0)
    partial = cross_products(
        block_regions, slot, incoming, side, genotypes, traits, nregion, nchunk
    )
    partial = partial.reshape((nsamp,) + partial.shape[2:])
    summed = lax.psum_scatter(partial, "samp", scatter_dimension=0, tiled=False)
    result = finish(block_regions, summed, traits, nlead, nregion, total)
    shared = lax.all_gather(result[:2], "samp", axis=0, tiled=False)
    shared = shared.reshape(nchunk, traits, 2, local_vars // nchunk)
    shared = jnp.transpose(shared, (2, 1, 0, 3)).reshape(2, traits, local_vars)
    return (shared[0], shared[1])


def solution(mesh):
    in_specs = (P("samp", "var"), P("samp", None), P("samp", None), P("var"), P())
    out_specs = (P(None, "var"), P(None, "var"))
    return jax.shard_map(body, mesh=mesh, in_specs=in_specs, out_specs=out_specs, check_vma=False)
```

time: 671 us -> 338 us (0.50)
  local copies, waits for them, and re-layouts: 181 us -> 5.94 us
  other arithmetic: 163 us -> 0.95 us
  matrix products: 63.3 us -> 0 us
  blocking collectives: 0 us -> 42 us
  loops' own time: 31.7 us -> 0 us
  Pallas kernels: 0 us -> 31.3 us
  waiting for transfers between devices: 209 us -> 238 us
    reduce_scatter x0 -> x1, waiting for transfers between devices: none -> 223 us  [body(): summed = lax.psum_scatter(partial, 'samp', scatter_dimension=0, tiled=False)]
    psum x2 -> x0, waiting for transfers between devices: 194 us -> none  [body(): cross, score, diag = lax.psum((cross, score, diag), 'samp')]
    another operation x12 -> x0, other arithmetic: 155 us -> none  [the longest x4 47.8 us: body(): chol = jnp.linalg.cholesky(gram)]
    dynamic_update_slice x24 -> x0, local copies, waits for them, and re-layouts: 113 us -> none  [body(): lax.map(block_cross, (jnp.arange(nblocks, dtype=jnp.int32), block_regions))]
    dot_general x30 -> x0, matrix products: 55.8 us -> none  [the longest x24 35.2 us: block_cross(): lax.dot_general(block_cols, chosen, (((0,), (0,)), ((), ())), preferred_e...]
    all_gather x0 -> x1, blocking collectives: none -> 42 us  [body(): shared = lax.all_gather(result[:2], 'samp', axis=0, tiled=False)]
    another operation x1 -> x0, loops' own time: 31.7 us -> none  [body(): lax.map(block_cross, (jnp.arange(nblocks, dtype=jnp.int32), block_regions))]
    pallas_call x0 -> x3, Pallas kernels: none -> 31.3 us  [the longest x1 13.6 us: cross_products(): pl.pallas_call(cross_kernel, grid_spec=pltpu.PrefetchScalarGridSpec(num_s...]
  transfers between devices with their start and end apart: 3 -> 2, of which waited for: 3 -> 2; matrix products, arithmetic and copies ran while one was open for 17% -> 0% of each run, Pallas kernels for 0% -> 0%
where the time goes in v1:
time: 338 us; the launch traced here: 337 us
  waiting for transfers between devices  238 us (70%)
  blocking collectives  42 us (12%)
  Pallas kernels  31.3 us (9%)
  between operations  14.1 us (4%)
  local copies, waits for them, and re-layouts  5.94 us (2%)
  starting transfers between devices  4.52 us (1%)
    reduce_scatter x1, waiting for transfers between devices, body(): summed = lax.psum_scatter(partial, 'samp', scatter_dimension=0, tiled=False)  223 us
    all_gather x1, blocking collectives, body(): shared = lax.all_gather(result[:2], 'samp', axis=0, tiled=False)  42 us
    all_to_all x1, waiting for transfers between devices, body(): lax.all_to_all(outgoing, 'var', split_axis=0, concat_axis=0, tiled=True)  14.5 us
    pallas_call x1, Pallas kernels, cross_products(): pl.pallas_call(cross_kernel, grid_spec=pltpu.PrefetchScalarGridSpec(num_s...  13.6 us
    pallas_call x1, Pallas kernels, gather(): pl.pallas_call(gather_kernel, grid=(samples // tile,), in_specs=[pl.Block...  10.6 us
    pallas_call x1, Pallas kernels, finish(): pl.pallas_call(functools.partial(finish_kernel, traits, total), in_specs=...  7.14 us
  transfers between devices with their start and end apart: 2, of which 2 were waited for; matrix products, arithmetic and copies ran while one was open for 0% of the time, Pallas kernels for 0%

profile of v1, /device:TPU:32, one launch (start us, length us, event | category | flops | bytes accessed | tf_op | source)
XLA Modules:
  0.0 336.8 jit_solution(14084964418800808801)
XLA Ops:
  7.2 0.0 copy-start.2
  7.2 0.0 copy-start.3
  7.2 0.0 copy-start.1
  7.2 1.4 reshape.102.listed_ref
  8.6 10.6 %lead_gather.1 = bf16[256,2048]{1,0:T(8,128)(2,1)} custom-call(s32[8,128]{1,0:T(8,128)} %reshape.102.listed_ref, bf16[2048,3072]{1,0:T(8,128)(2,1)} %geno_ref.3), custom_call_target="tpu_custom_call" | custom-call | tf_op jit(solution)/shard_map/lead_gather/pallas_call | solution.py:57
  19.1 4.5 %all-to-all-start = ((bf16[8,32,2048]{2,1,0:T(8,128)(2,1)}), bf16[8,32,2048]{2,1,0:T(8,128)(2,1)S(1)}, u32[]{:S(2)}, u32[]{:S(2)}) async-start(bf16[8,32,2048]{2,1,0:T(8,128)(2,1)} %bitcast.30), calls=%async_computation | async-start | bytes 2097152 | tf_op jit(solution)/shard_map/all_to_all | solution.py:242
  23.6 0.0 reduce-scatter.2.cloned.1.call-start
  23.7 0.7 bitcast_select_fusion
  24.4 0.1 copy.26
  24.5 0.2 convert_reduce_fusion
  24.7 0.1 copy.29
  24.8 0.1 copy.25
  24.9 0.0 copy-done.2
  25.0 0.0 copy-done.3
  25.0 0.1 pad_maximum_fusion.side_ref
  25.1 14.5 %all-to-all-done = bf16[8,32,2048]{2,1,0:T(8,128)(2,1)S(1)} async-done(((bf16[8,32,2048]{2,1,0:T(8,128)(2,1)}), bf16[8,32,2048]{2,1,0:T(8,128)(2,1)S(1)}, u32[]{:S(2)}, u32[]{:S(2)}) %all-to-all-start) | async-done | bytes 1048608 | tf_op jit(solution)/shard_map/all_to_all | solution.py:242
  39.6 0.0 copy-done.1
  39.6 13.6 %cross_products.1 = f32[8,4,72,512]{3,2,1,0:T(8,128)S(1)} custom-call(s32[24]{0:T(128)S(1)} %copy-done.1, s32[128,1]{1,0:T(8,128)S(1)} %fusion.1.slot_ref, bf16[256,2048]{1,0:T(8,128)(2,1)S(1)} %bitcast.29, bf16[32,2048]{1,0:T(8,128)(2,1)S(1)} %pad_maximum_fusion.side_ref, bf16[2048,3072]{1,0:T(8,128)(2,1)} %geno_ref.3), custom_call_target="tpu_custom_call" | custom-call | tf_op jit(solution)/shard_map/cross_products/pallas_call | solution.py:137
  53.2 0.0 copy-start
  53.2 2.1 copy-done
  55.3 0.0 reduce-scatter.2.cloned.1.call-update
  55.3 223.3 %reduce-scatter.2.cloned.1.call-done = f32[1,72,512]{2,1,0:T(8,128)} async-done(((f32[32,72,512]{2,1,0:T(8,128)}), f32[1,72,512]{2,1,0:T(8,128)}) %reduce-scatter.2.cloned.1.call-update) | async-done | bytes 147472 | tf_op jit(solution)/shard_map/reduce_scatter | solution.py:254
  278.7 7.1 %conditional_finish.1 = f32[8,384]{1,0:T(8,128)} custom-call(s32[24]{0:T(128)} %region_ref.3, f32[72,512]{1,0:T(8,128)} %bitcast.32), custom_call_target="tpu_custom_call" | custom-call | tf_op jit(solution)/shard_map/conditional_finish/pallas_call | solution.py:212
  285.8 0.7 slice_bitcast_fusion
  286.5 42.0 %all-gather.1 = f32[32,2,384]{2,1,0:T(2,128)S(1)} all-gather(f32[1,2,384]{2,1,0:T(2,128)S(1)} %slice_bitcast_fusion), channel_id=2, replica_groups=mesh['samp'=32,'var'=8] {'samp'}, dimensions={0}, use_global_device_ids=true | all-gather | bytes 101376 | tf_op jit(solution)/shard_map/all_gather | solution.py:256
  328.6 0.1 fusion.4
  328.7 0.6 copy.33
  329.3 0.6 copy.32
  (4 shorter events, 0.0 us)
Async XLA Ops:
  7.2 17.8 %copy-start.2 = (bf16[2048,4]{0,1:T(4,128)(2,1)S(1)}, bf16[2048,4]{0,1:T(4,128)(2,1)}, u32[]{:S(2)}) copy-start(bf16[2048,4]{0,1:T(4,128)(2,1)} %param.7) | copy-start | bytes 49156
  7.2 17.8 %copy-start.3 = (bf16[2048,4]{0,1:T(4,128)(2,1)S(1)}, bf16[2048,4]{0,1:T(4,128)(2,1)}, u32[]{:S(2)}) copy-start(bf16[2048,4]{0,1:T(4,128)(2,1)} %param.6) | copy-start | bytes 49156
  7.2 32.4 %copy-start.1 = (s32[24]{0:T(128)S(1)}, s32[24]{0:T(128)}, u32[]{:S(2)}) copy-start(s32[24]{0:T(128)} %region_ref.3) | copy-start | bytes 292
  19.1 20.4 %all-to-all-start = ((bf16[8,32,2048]{2,1,0:T(8,128)(2,1)}), bf16[8,32,2048]{2,1,0:T(8,128)(2,1)S(1)}, u32[]{:S(2)}, u32[]{:S(2)}) async-start(bf16[8,32,2048]{2,1,0:T(8,128)(2,1)} %bitcast.30), calls=%async_computation | async-start | bytes 2097152 | tf_op jit(solution)/shard_map/all_to_all | solution.py:242
  23.6 255.1 %reduce-scatter.2.cloned.1.call-start = ((), (), s32[]{:S(2)}) async-start(), calls=%async_computation.2 | async-start | bytes 4866048 | tf_op jit(solution)/shard_map/reduce_scatter | solution.py:254
  53.2 2.1 copy-start
Sparse Core Ops, SparseCore 0:
  55.5 223.1 reduce-scatter.1

commit v2 on v1

--- a/solution.py
+++ b/solution.py
@@ -68,7 +68,18 @@
     )(listed, genotypes)
 
 
-def cross_kernel(region_ref, slot_ref, incoming_ref, side_ref, geno_ref, out_ref, lead, weighted, gram):
+def cross_kernel(
+    region_ref,
+    slot_ref,
+    incoming_ref,
+    side_ref,
+    geno_ref,
+    cross_ref,
+    small_ref,
+    gram_ref,
+    lead,
+    weighted,
+):
     nregion, rows, samples = weighted.shape
     nlead = lead.shape[0] // nregion
     traits = (rows - EXTRA) // nlead
@@ -92,14 +103,21 @@
                     jnp.bfloat16
                 )
             weighted[region, traits * nlead :, :] = side_ref[:EXTRA, :]
-            gram[region] = lax.dot_general(
+            gram = lax.dot_general(
                 weighted[region],
                 lead[region * nlead : (region + 1) * nlead, :],
                 NT,
                 preferred_element_type=jnp.float32,
             )
+            there = slice(region * nlead, (region + 1) * nlead)
+            last = traits * nlead
+            for trait in range(traits):
+                gram_ref[trait, :nlead, there] = gram[trait * nlead : (trait + 1) * nlead, :]
+                gram_ref[trait, nlead : nlead + 1, there] = gram[last + trait : last + trait + 1, :]
+                gram_ref[trait, nlead + 1 :, there] = jnp.zeros((7, nlead), jnp.float32)
 
     per_chunk = chunk // VB
+    small_ref[...] = jnp.zeros_like(small_ref)
     for block in range(per_chunk):
         region = region_ref[step * per_chunk + block]
         cols = geno_ref[:, block * VB : (block + 1) * VB]
@@ -110,21 +128,14 @@
             side_ref[EXTRA:, :], square, NN, preferred_element_type=jnp.float32
         )
         here = slice(block * VB, (block + 1) * VB)
+        last = traits * nlead
+        other = per_chunk + block
         for trait in range(traits):
-            out_ref[0, trait, :nlead, here] = acc[trait * nlead : (trait + 1) * nlead, :]
-            out_ref[0, trait, nlead : nlead + 1, here] = acc[
-                traits * nlead + trait : traits * nlead + trait + 1, :
-            ]
-            out_ref[0, trait, nlead + 1 : nlead + 2, here] = diag[trait : trait + 1, :]
-            out_ref[0, trait, nlead + 2 :, here] = jnp.zeros((6, VB), jnp.float32)
-    for trait in range(traits):
-        out_ref[0, trait, nlead:, chunk:] = jnp.zeros((8, 2 * nlead), jnp.float32)
-        for region in range(nregion):
-            there = slice(chunk + region * nlead, chunk + (region + 1) * nlead)
-            out_ref[0, trait, :nlead, there] = gram[region, trait * nlead : (trait + 1) * nlead, :]
-            out_ref[0, trait, nlead : nlead + 1, there] = gram[
-                region, traits * nlead + trait : traits * nlead + trait + 1, :
-            ]
+            cross_ref[trait, 0, :, here] = acc[trait * nlead : (trait + 1) * nlead, :].astype(
+                jnp.bfloat16
+            )
+            small_ref[trait, 0, block : block + 1, :] = acc[last + trait : last + trait + 1, :]
+            small_ref[trait, 0, other : other + 1, :] = diag[trait : trait + 1, :]
 
 
 def cross_products(regions, slot, incoming, side, genotypes, traits, nregion, nchunk):
@@ -133,7 +144,6 @@
     chunk = local_vars // nchunk
     rows = traits * nlead + EXTRA
     whole = lambda i, r: (0, 0)
-    shape = (nchunk, traits, nlead + 8, chunk + nregion * nlead)
     return pl.pallas_call(
         cross_kernel,
         grid_spec=pltpu.PrefetchScalarGridSpec(
@@ -145,22 +155,240 @@
                 pl.BlockSpec(side.shape, whole),
                 pl.BlockSpec((samples, chunk), lambda i, r: (0, i)),
             ],
-            out_specs=pl.BlockSpec((1,) + shape[1:], lambda i, r: (i, 0, 0, 0)),
+            out_specs=[
+                pl.BlockSpec((traits, 1, nlead, chunk), lambda i, r: (0, i, 0, 0)),
+                pl.BlockSpec((traits, 1, 8, VB), lambda i, r: (0, i, 0, 0)),
+                pl.BlockSpec((traits, nlead + 8, nregion * nlead), lambda i, r: (0, 0, 0)),
+            ],
             scratch_shapes=[
                 pltpu.VMEM((nregion * nlead, samples), jnp.bfloat16),
                 pltpu.VMEM((nregion, rows, samples), jnp.bfloat16),
-                pltpu.VMEM((nregion, rows, nlead), jnp.float32),
             ],
         ),
-        out_shape=jax.ShapeDtypeStruct(shape, jnp.float32),
+        out_shape=[
+            jax.ShapeDtypeStruct((traits, nchunk, nlead, chunk), jnp.bfloat16),
+            jax.ShapeDtypeStruct((traits, nchunk, 8, VB), jnp.float32),
+            jax.ShapeDtypeStruct((traits, nlead + 8, nregion * nlead), jnp.float32),
+        ],
         compiler_params=pltpu.CompilerParams(vmem_limit_bytes=48 * 1024 * 1024),
         name="cross_products",
     )(regions, slot, incoming, side, genotypes)
 
 
-def finish_kernel(traits, total, region_ref, sum_ref, out_ref, inverse, pivots, target):
+def meet(peers):
+    barrier = pltpu.get_barrier_semaphore()
+    for peer in peers:
+        pl.semaphore_signal(
+            barrier, inc=1, device_id={"samp": peer}, device_id_type=pl.DeviceIdType.MESH
+        )
+    pl.semaphore_wait(barrier, len(peers))
+
+
+def places(nx, nz):
+    me = lax.axis_index("samp")
+    x, z = lax.rem(me, nx), lax.div(me, nx)
+    xpeers = [z * nx + lax.rem(x + d, nx) for d in range(1, nx)]
+    zpeers = [lax.rem(z + d, nz) * nx + x for d in range(1, nz)]
+    return x, z, xpeers, zpeers
+
+
+def reduce_kernel(
+    cross_ref,
+    small_ref,
+    gram_ref,
+    cross_out,
+    small_out,
+    gram_out,
+    x_cross,
+    x_small,
+    x_gram,
+    mid_cross,
+    mid_small,
+    mid_gram,
+    z_cross,
+    z_small,
+    z_gram,
+    sent,
+    got,
+):
+    nx, nz = cross_ref.shape[:2]
+    x, z, xpeers, zpeers = places(nx, nz)
+    meet(xpeers + zpeers)
+    started = []
+
+    def push(source, target, peer):
+        count = len(started)
+        copy = pltpu.make_async_remote_copy(
+            src_ref=source,
+            dst_ref=target,
+            send_sem=sent.at[count],
+            recv_sem=got.at[count],
+            device_id={"samp": peer},
+            device_id_type=pl.DeviceIdType.MESH,
+        )
+        copy.start()
+        started.append(copy)
+        return copy
+
+    order = sorted(range(1, nz), key=lambda d: -min(d, nz - d)) + [0]
+    early = []
+    for i, peer in enumerate(xpeers):
+        trait = lax.rem(x + i + 1, nx)
+        early.append(push(gram_ref.at[trait], x_gram.at[i], peer))
+        early.append(push(small_ref.at[trait], x_small.at[i], peer))
+    chunks = {}
+    for d in order:
+        chunk = lax.rem(z + d, nz)
+        chunks[d] = [
+            push(cross_ref.at[lax.rem(x + i + 1, nx), chunk], x_cross.at[i, d], peer)
+            for i, peer in enumerate(xpeers)
+        ]
+    for copy in early:
+        copy.wait_recv()
+    mid_gram[...] = gram_ref[x] + x_gram[0] + x_gram[1] + x_gram[2]
+    mid_small[...] = small_ref[x] + x_small[0] + x_small[1] + x_small[2]
+    late = []
+    for d in order:
+        chunk = lax.rem(z + d, nz)
+        if d > 0:
+            peer = zpeers[d - 1]
+            late.append(push(mid_gram, z_gram.at[d - 1], peer))
+            late.append(push(mid_small.at[chunk], z_small.at[d - 1], peer))
+        for copy in chunks[d]:
+            copy.wait_recv()
+        total = cross_ref[x, chunk].astype(jnp.float32)
+        for i in range(nx - 1):
+            total = total + x_cross[i, d].astype(jnp.float32)
+        if d > 0:
+            mid_cross[d] = total.astype(jnp.bfloat16)
+            late.append(push(mid_cross.at[d], z_cross.at[d - 1], zpeers[d - 1]))
+        else:
+            cross_out[...] = total
+    for copy in late:
+        copy.wait_recv()
+    gram = mid_gram[...]
+    small = mid_small[z]
+    cross = cross_out[...]
+    for d in range(nz - 1):
+        gram = gram + z_gram[d]
+        small = small + z_small[d]
+        cross = cross + z_cross[d].astype(jnp.float32)
+    gram_out[...] = gram
+    small_out[...] = small
+    cross_out[...] = cross
+    for copy in started:
+        copy.wait_send()
+
+
+def reduce_over_samples(cross, small, gram):
+    nx, nz = cross.shape[:2]
+    count = 2 * (nx - 1) + nz * (nx - 1) + 3 * (nz - 1)
+    vmem = pl.BlockSpec(memory_space=pltpu.VMEM)
+    lands = lambda lead, array, skip: pltpu.VMEM(lead + array.shape[skip:], array.dtype)
+    return pl.pallas_call(
+        reduce_kernel,
+        in_specs=[vmem] * 3,
+        out_specs=[vmem] * 3,
+        out_shape=[
+            jax.ShapeDtypeStruct(cross.shape[2:], jnp.float32),
+            jax.ShapeDtypeStruct(small.shape[2:], jnp.float32),
+            jax.ShapeDtypeStruct(gram.shape[1:], jnp.float32),
+        ],
+        scratch_shapes=[
+            lands((nx - 1, nz), cross, 2),
+            lands((nx - 1, nz), small, 2),
+            lands((nx - 1,), gram, 1),
+            lands((nz,), cross, 2),
+            lands((nz,), small, 2),
+            lands((), gram, 1),
+            lands((nz - 1,), cross, 2),
+            lands((nz - 1,), small, 2),
+            lands((nz - 1,), gram, 1),
+            pltpu.SemaphoreType.DMA((count,)),
+            pltpu.SemaphoreType.DMA((count,)),
+        ],
+        compiler_params=pltpu.CompilerParams(collective_id=0, has_side_effects=True),
+        name="reduce_over_samples",
+    )(cross, small, gram)
+
+
+def share_kernel(nx, nz, result_ref, scores_ref, variances_ref, lane, whole, sent, got, here_sem):
+    x, z, xpeers, zpeers = places(nx, nz)
+    meet(xpeers + zpeers)
+    own = pltpu.make_async_copy(result_ref, lane.at[z], here_sem.at[0])
+    own.start()
+    first = []
+    for i, peer in enumerate(zpeers):
+        copy = pltpu.make_async_remote_copy(
+            src_ref=result_ref,
+            dst_ref=lane.at[z],
+            send_sem=sent.at[i],
+            recv_sem=got.at[i],
+            device_id={"samp": peer},
+            device_id_type=pl.DeviceIdType.MESH,
+        )
+        copy.start()
+        first.append(copy)
+    own.wait()
+    for copy in first:
+        copy.wait_recv()
+    mine = pltpu.make_async_copy(lane, whole.at[x], here_sem.at[1])
+    mine.start()
+    second = []
+    for i, peer in enumerate(xpeers):
+        copy = pltpu.make_async_remote_copy(
+            src_ref=lane,
+            dst_ref=whole.at[x],
+            send_sem=sent.at[nz - 1 + i],
+            recv_sem=got.at[nz - 1 + i],
+            device_id={"samp": peer},
+            device_id_type=pl.DeviceIdType.MESH,
+        )
+        copy.start()
+        second.append(copy)
+    mine.wait()
+    for copy in second:
+        copy.wait_recv()
+    per_chunk = scores_ref.shape[1] // (nz * VB)
+    for trait in range(nx):
+        for chunk in range(nz):
+            tile = whole[trait, chunk]
+            for block in range(per_chunk):
+                at = (chunk * per_chunk + block) * VB
+                scores_ref[trait : trait + 1, at : at + VB] = tile[block : block + 1, :]
+                variances_ref[trait : trait + 1, at : at + VB] = tile[
+                    per_chunk + block : per_chunk + block + 1, :
+                ]
+    for copy in first + second:
+        copy.wait_send()
+
+
+def share(result, nx, nz, local_vars):
+    vmem = pl.BlockSpec(memory_space=pltpu.VMEM)
+    out = jax.ShapeDtypeStruct((nx, local_vars), jnp.float32)
+    count = nx + nz - 2
+    return pl.pallas_call(
+        functools.partial(share_kernel, nx, nz),
+        in_specs=[vmem],
+        out_specs=[vmem] * 2,
+        out_shape=[out, out],
+        scratch_shapes=[
+            pltpu.VMEM((nz,) + result.shape, jnp.float32),
+            pltpu.VMEM((nx, nz) + result.shape, jnp.float32),
+            pltpu.SemaphoreType.DMA((count,)),
+            pltpu.SemaphoreType.DMA((count,)),
+            pltpu.SemaphoreType.DMA((2,)),
+        ],
+        compiler_params=pltpu.CompilerParams(collective_id=1, has_side_effects=True),
+        name="share_results",
+    )(result)
+
+
+def finish_kernel(
+    traits, total, region_ref, cross_ref, small_ref, gram_ref, out_ref, inverse, pivots, target
+):
     nregion, nlead, _ = inverse.shape
-    chunk = out_ref.shape[1]
+    chunk = cross_ref.shape[1]
     per_chunk = chunk // VB
     first = (lax.axis_index("samp") // traits) * per_chunk
     eye = (
@@ -171,7 +399,7 @@
     below = lax.broadcasted_iota(jnp.int32, (nlead, 1), 0)
     state = [
         jnp.concatenate(
-            [sum_ref[:nlead, chunk + r * nlead : chunk + (r + 1) * nlead], unit], axis=1
+            [gram_ref[:nlead, r * nlead : (r + 1) * nlead], unit], axis=1
         )
         for r in range(nregion)
     ]
@@ -185,7 +413,7 @@
         upper = state[r][:, :nlead]
         inverse[r] = lower
         pivot = 1.0 / jnp.sum(jnp.where(eye, upper, 0.0), axis=1, keepdims=True)
-        score = sum_ref[nlead : nlead + 1, chunk + r * nlead : chunk + (r + 1) * nlead]
+        score = gram_ref[nlead : nlead + 1, r * nlead : (r + 1) * nlead]
         pivots[r] = jnp.broadcast_to(pivot, (nlead, VB))
         target[r] = jnp.broadcast_to(
             jnp.sum(lower * score, axis=1, keepdims=True) * pivot, (nlead, VB)
@@ -196,34 +424,37 @@
         region = region_ref[first + block]
         solved = lax.dot_general(
             inverse[region],
-            sum_ref[:nlead, here],
+            cross_ref[:, here],
             NN,
             preferred_element_type=jnp.float32,
             precision=lax.Precision.HIGHEST,
         )
         fit = jnp.sum(solved * target[region], axis=0, keepdims=True)
         used = jnp.sum(solved * solved * pivots[region], axis=0, keepdims=True)
-        out_ref[0:1, here] = (sum_ref[nlead : nlead + 1, here] - fit) / math.sqrt(total)
-        out_ref[1:2, here] = (sum_ref[nlead + 1 : nlead + 2, here] - used) / total
-
-
-def finish(regions, summed, traits, nlead, nregion, total):
-    chunk = summed.shape[1] - nregion * nlead
+        other = per_chunk + block
+        out_ref[block : block + 1, :] = (small_ref[block : block + 1, :] - fit) / math.sqrt(total)
+        out_ref[other : other + 1, :] = (small_ref[other : other + 1, :] - used) / total
+
+
+def finish(regions, cross, small, gram, traits, nlead, nregion, total):
+    vmem = pl.BlockSpec(memory_space=pltpu.VMEM)
     return pl.pallas_call(
         functools.partial(finish_kernel, traits, total),
         in_specs=[
             pl.BlockSpec(memory_space=pltpu.SMEM),
-            pl.BlockSpec(memory_space=pltpu.VMEM),
+            vmem,
+            vmem,
+            vmem,
         ],
         out_specs=pl.BlockSpec(memory_space=pltpu.VMEM),
-        out_shape=jax.ShapeDtypeStruct((8, chunk), jnp.float32),
+        out_shape=jax.ShapeDtypeStruct(small.shape, jnp.float32),
         scratch_shapes=[
             pltpu.VMEM((nregion, nlead, nlead), jnp.float32),
             pltpu.VMEM((nregion, nlead, VB), jnp.float32),
             pltpu.VMEM((nregion, nlead, VB), jnp.float32),
         ],
         name="conditional_finish",
-    )(regions, summed)
+    )(regions, cross, small, gram)
 
 
 def body(genotypes, residuals, weights, block_regions, leads):
@@ -250,13 +481,10 @@
     partial = cross_products(
         block_regions, slot, incoming, side, genotypes, traits, nregion, nchunk
     )
-    partial = partial.reshape((nsamp,) + partial.shape[2:])
-    summed = lax.psum_scatter(partial, "samp", scatter_dimension=0, tiled=False)
-    result = finish(block_regions, summed, traits, nlead, nregion, total)
-    shared = lax.all_gather(result[:2], "samp", axis=0, tiled=False)
-    shared = shared.reshape(nchunk, traits, 2, local_vars // nchunk)
-    shared = jnp.transpose(shared, (2, 1, 0, 3)).reshape(2, traits, local_vars)
-    return (shared[0], shared[1])
+    cross, small, gram = reduce_over_samples(*partial)
+    result = finish(block_regions, cross, small, gram, traits, nlead, nregion, total)
+    scores, variances = share(result, traits, nchunk, local_vars)
+    return (scores, variances)
 
 
 def solution(mesh):

time: 338 us -> 107 us (0.32)
  waiting for transfers between devices: 238 us -> 14.6 us
  Pallas kernels: 31.3 us -> 78.6 us
  blocking collectives: 42 us -> 0 us
  between operations: 14.1 us -> 0.74 us
    reduce_scatter x1 -> x0, waiting for transfers between devices: 223 us -> none  [body(): summed = lax.psum_scatter(partial, 'samp', scatter_dimension=0, tiled=False)]
    pallas_call x0 -> x2, Pallas kernels: none -> 47.2 us  [the longest x1 34.7 us: reduce_over_samples(): pl.pallas_call(reduce_kernel, in_specs=[vmem] * 3, out_specs=[vmem] * 3,...]
    all_gather x1 -> x0, blocking collectives: 42 us -> none  [body(): shared = lax.all_gather(result[:2], 'samp', axis=0, tiled=False)]
  transfers between devices with their start and end apart: 2 -> 1, of which waited for: 2 -> 1; matrix products, arithmetic and copies ran while one was open for 0% -> 1% of each run, Pallas kernels for 0% -> 0%
where the time goes in v2:
time: 107 us; the launch traced here: 106 us
  Pallas kernels  78.6 us (73%)
  waiting for transfers between devices  14.6 us (14%)
  local copies, waits for them, and re-layouts  7.05 us (7%)
  starting transfers between devices  4.47 us (4%)
    pallas_call x1, Pallas kernels, reduce_over_samples(): pl.pallas_call(reduce_kernel, in_specs=[vmem] * 3, out_specs=[vmem] * 3,...  34.7 us
    all_to_all x1, waiting for transfers between devices, body(): lax.all_to_all(outgoing, 'var', split_axis=0, concat_axis=0, tiled=True)  14.6 us
    pallas_call x1, Pallas kernels, cross_products(): pl.pallas_call(cross_kernel, grid_spec=pltpu.PrefetchScalarGridSpec(num_s...  13.7 us
    pallas_call x1, Pallas kernels, share(): pl.pallas_call(functools.partial(share_kernel, nx, nz), in_specs=[vmem],...  12.6 us
    pallas_call x1, Pallas kernels, gather(): pl.pallas_call(gather_kernel, grid=(samples // tile,), in_specs=[pl.Block...  10.6 us
    pallas_call x1, Pallas kernels, finish(): pl.pallas_call(functools.partial(finish_kernel, traits, total), in_specs=...  7.12 us
    unnamed x14, local copies, waits for them, and re-layouts  5.3 us
    all_to_all x1, starting transfers between devices, body(): lax.all_to_all(outgoing, 'var', split_axis=0, concat_axis=0, tiled=True)  4.47 us
  transfers between devices with their start and end apart: 1, of which 1 were waited for; matrix products, arithmetic and copies ran while one was open for 1% of the time, Pallas kernels for 0%

profile of v2, /device:TPU:32, one launch (start us, length us, event | category | flops | bytes accessed | tf_op | source)
XLA Modules:
  0.0 106.4 jit_solution(5637729443610056544)
XLA Ops:
  0.6 0.0 copy-start.4
  0.6 0.0 copy-start.5
  0.7 0.0 copy-start.3
  0.7 1.4 %reshape.91.listed_ref = s32[8,128]{1,0:T(8,128)} reshape(s32[16,64]{1,0:T(8,128)} %param.9) | data formatting | bytes 8192 | tf_op jit(solution)/shard_map/reshape | solution.py:471
  2.0 10.6 %lead_gather.1 = bf16[256,2048]{1,0:T(8,128)(2,1)} custom-call(s32[8,128]{1,0:T(8,128)} %reshape.91.listed_ref, bf16[2048,3072]{1,0:T(8,128)(2,1)} %geno_ref.3), custom_call_target="tpu_custom_call" | custom-call | tf_op jit(solution)/shard_map/lead_gather/pallas_call | solution.py:57
  12.6 4.5 %all-to-all-start = ((bf16[8,32,2048]{2,1,0:T(8,128)(2,1)}), bf16[8,32,2048]{2,1,0:T(8,128)(2,1)S(1)}, u32[]{:S(2)}, u32[]{:S(2)}) async-start(bf16[8,32,2048]{2,1,0:T(8,128)(2,1)} %bitcast.14), calls=%async_computation | async-start | bytes 2097152 | tf_op jit(solution)/shard_map/all_to_all | solution.py:473
  17.1 0.7 bitcast_select_fusion
  17.8 0.1 copy.16
  17.9 0.2 convert_reduce_fusion
  18.1 0.1 copy.19
  18.2 0.1 copy.15
  18.3 0.0 copy-done.4
  18.3 0.0 copy-done.5
  18.4 0.1 pad_maximum_fusion.side_ref
  18.4 14.6 %all-to-all-done = bf16[8,32,2048]{2,1,0:T(8,128)(2,1)S(1)} async-done(((bf16[8,32,2048]{2,1,0:T(8,128)(2,1)}), bf16[8,32,2048]{2,1,0:T(8,128)(2,1)S(1)}, u32[]{:S(2)}, u32[]{:S(2)}) %all-to-all-start) | async-done | bytes 1048608 | tf_op jit(solution)/shard_map/all_to_all | solution.py:473
  33.0 0.0 copy-done.3
  33.0 13.7 %cross_products.1 = (bf16[4,8,64,384]{3,2,1,0:T(8,128)(2,1)S(1)}, f32[4,8,8,128]{3,2,1,0:T(8,128)S(1)}, f32[4,72,128]{2,1,0:T(8,128)S(1)}) custom-call(s32[24]{0:T(128)S(1)} %copy-done.3, s32[128,1]{1,0:T(8,128)S(1)} %fusion.1.slot_ref, bf16[256,2048]{1,0:T(8,128)(2,1)S(1)} %bitcast.13, bf16[32,2048]{1,0:T(8,128)(2,1)S(1)} %pad_maximum_fusion.side_ref, ...), custom_call_target="tpu_custom_call" | custom-call | tf_op jit(solution)/shard_map/cross_products/pallas_call | solution.py:147
  46.8 0.0 copy-start
  46.8 1.1 %copy-done = bf16[4,8,64,384]{3,2,1,0:T(8,128)(2,1)} copy-done((bf16[4,8,64,384]{3,2,1,0:T(8,128)(2,1)}, bf16[4,8,64,384]{3,2,1,0:T(8,128)(2,1)S(1)}, u32[]{:S(2)}) %copy-start) | copy-done | bytes 1572888
  47.9 0.0 copy-start.1
  47.9 0.7 copy-done.1
  48.6 0.0 copy-start.2
  48.6 0.7 copy-done.2
  49.2 34.7 %reduce_over_samples.1 = (f32[64,384]{1,0:T(8,128)}, f32[8,128]{1,0:T(8,128)}, f32[72,128]{1,0:T(8,128)}) custom-call(bf16[4,8,64,384]{3,2,1,0:T(8,128)(2,1)} %copy-done, f32[4,8,8,128]{3,2,1,0:T(8,128)} %copy-done.2, f32[4,72,128]{2,1,0:T(8,128)} %copy-done.1), custom_call_target="tpu_custom_call" | custom-call | tf_op jit(solution)/shard_map/reduce_over_samples/pallas_call | solution.py:288
  83.9 7.1 %conditional_finish.1.result_ref = f32[8,128]{1,0:T(8,128)} custom-call(s32[24]{0:T(128)} %region_ref.3, f32[64,384]{1,0:T(8,128)} %get-tuple-element.11.cross_ref, f32[8,128]{1,0:T(8,128)} %get-tuple-element.12.small_ref, f32[72,128]{1,0:T(8,128)} %get-tuple-element.13.gram_ref), custom_call_target="tpu_custom_call" | custom-call | tf_op jit(solution)/shard_map/conditional_finish/pallas_call | solution.py:441
  91.0 12.6 %share_results.1 = (f32[4,3072]{1,0:T(4,128)}, f32[4,3072]{1,0:T(4,128)}) custom-call(f32[8,128]{1,0:T(8,128)} %conditional_finish.1.result_ref), custom_call_target="tpu_custom_call" | custom-call | tf_op jit(solution)/shard_map/share_results/pallas_call | solution.py:370
  103.6 1.4 %copy.22 = f32[4,3072]{1,0:T(4,128)} copy(f32[4,3072]{1,0:T(4,128)} %get-tuple-element.19) | data formatting | bytes 98304
  105.0 1.4 %copy.23 = f32[4,3072]{1,0:T(4,128)} copy(f32[4,3072]{1,0:T(4,128)} %get-tuple-element.20) | data formatting | bytes 98304
  (3 shorter events, 0.0 us)
Async XLA Ops:
  0.6 17.7 %copy-start.4 = (bf16[2048,4]{0,1:T(4,128)(2,1)S(1)}, bf16[2048,4]{0,1:T(4,128)(2,1)}, u32[]{:S(2)}) copy-start(bf16[2048,4]{0,1:T(4,128)(2,1)} %param.7) | copy-start | bytes 49156
  0.6 17.7 %copy-start.5 = (bf16[2048,4]{0,1:T(4,128)(2,1)S(1)}, bf16[2048,4]{0,1:T(4,128)(2,1)}, u32[]{:S(2)}) copy-start(bf16[2048,4]{0,1:T(4,128)(2,1)} %param.6) | copy-start | bytes 49156
  0.7 32.4 %copy-start.3 = (s32[24]{0:T(128)S(1)}, s32[24]{0:T(128)}, u32[]{:S(2)}) copy-start(s32[24]{0:T(128)} %region_ref.3) | copy-start | bytes 292
  12.6 20.4 %all-to-all-start = ((bf16[8,32,2048]{2,1,0:T(8,128)(2,1)}), bf16[8,32,2048]{2,1,0:T(8,128)(2,1)S(1)}, u32[]{:S(2)}, u32[]{:S(2)}) async-start(bf16[8,32,2048]{2,1,0:T(8,128)(2,1)} %bitcast.14), calls=%async_computation | async-start | bytes 2097152 | tf_op jit(solution)/shard_map/all_to_all | solution.py:473
  46.8 1.1 %copy-start = (bf16[4,8,64,384]{3,2,1,0:T(8,128)(2,1)}, bf16[4,8,64,384]{3,2,1,0:T(8,128)(2,1)S(1)}, u32[]{:S(2)}) copy-start(bf16[4,8,64,384]{3,2,1,0:T(8,128)(2,1)S(1)} %get-tuple-element.8.cross_ref) | copy-start | bytes 4718596
  47.9 0.7 copy-start.1
  48.6 0.7 copy-start.2

commit v3 on v2

v3 whole, which is shorter than its diff:
```python
import functools
import math

import jax
import jax.numpy as jnp
from jax import lax
from jax.experimental import pallas as pl
from jax.experimental.pallas import tpu as pltpu
from jax.sharding import PartitionSpec as P

VB = 128
HOST = 32
NT = (((1,), (1,)), ((), ()))
NN = (((1,), (0,)), ((), ()))
EXTRA = 16


def greet(axis, peers):
    barrier = pltpu.get_barrier_semaphore()
    for peer in peers:
        pl.semaphore_signal(
            barrier, inc=1, device_id={axis: peer}, device_id_type=pl.DeviceIdType.MESH
        )


def hear(peers):
    pl.semaphore_wait(pltpu.get_barrier_semaphore(), len(peers))


def meet(peers):
    greet("samp", peers)
    hear(peers)


def gather_kernel(listed_ref, geno_ref, out_ref, onehot, leaving, landed, sent, got):
    nvar, slots = listed_ref.shape
    local_vars = geno_ref.shape[1]
    tile = geno_ref.shape[0]
    ntile = leaving.shape[0]
    step = pl.program_id(0)
    me = lax.axis_index("var")
    peers = [lax.rem(me + d, nvar) for d in range(1, nvar)]

    @pl.when(step == 0)
    def _():
        greet("var", peers)
        base = me * local_vars
        offset = listed_ref[...] - base
        hosted = (offset >= 0) & (offset < local_vars)
        before = lax.broadcasted_iota(jnp.int32, (slots, slots), 0) < lax.broadcasted_iota(
            jnp.int32, (slots, slots), 1
        )
        rank = lax.dot_general(
            hosted.astype(jnp.float32),
            before.astype(jnp.float32),
            NN,
            preferred_element_type=jnp.float32,
        ).astype(jnp.int32)
        rank = jnp.where(hosted, rank, HOST)
        place = lax.broadcasted_iota(jnp.int32, (HOST, slots), 0)
        lanes = lax.broadcasted_iota(jnp.int32, (HOST, local_vars), 1)
        for owner in range(nvar):
            match = rank[owner : owner + 1, :] == place
            picked = jnp.sum(
                jnp.where(match, offset[owner : owner + 1, :], 0), axis=1, keepdims=True
            )
            onehot[owner * HOST : (owner + 1) * HOST, :] = (
                (lanes == picked).astype(jnp.float32).astype(jnp.bfloat16)
            )
        hear(peers)

    found = lax.dot_general(
        onehot[...], geno_ref[...], NT, preferred_element_type=jnp.float32
    ).astype(jnp.bfloat16)
    for owner in range(nvar):
        leaving[step, owner] = found[owner * HOST : (owner + 1) * HOST, :]

    def copy_to(turn, i):
        return pltpu.make_async_remote_copy(
            src_ref=leaving.at[turn, peers[i]],
            dst_ref=landed.at[turn, i],
            send_sem=sent.at[turn, i],
            recv_sem=got.at[turn, i],
            device_id={"var": peers[i]},
            device_id_type=pl.DeviceIdType.MESH,
        )

    for i in range(nvar - 1):
        copy_to(step, i).start()

    @pl.when(step == ntile - 1)
    def _():
        for turn in range(ntile):
            at = slice(turn * tile, (turn + 1) * tile)
            out_ref[me, :, at] = leaving[turn, me]
            for i in range(nvar - 1):
                copy_to(turn, i).wait_recv()
                out_ref[lax.rem(me + nvar - 1 - i, nvar), :, at] = landed[turn, i]
        for turn in range(ntile):
            for i in range(nvar - 1):
                copy_to(turn, i).wait_send()


def gather(listed, genotypes, tile=256):
    samples, local_vars = genotypes.shape
    nvar, slots = listed.shape
    rows = nvar * HOST
    ntile = samples // tile
    found = pl.pallas_call(
        gather_kernel,
        grid=(ntile,),
        in_specs=[
            pl.BlockSpec((nvar, slots), lambda i: (0, 0)),
            pl.BlockSpec((tile, local_vars), lambda i: (i, 0)),
        ],
        out_specs=pl.BlockSpec((nvar, HOST, samples), lambda i: (0, 0, 0)),
        out_shape=jax.ShapeDtypeStruct((nvar, HOST, samples), jnp.bfloat16),
        scratch_shapes=[
            pltpu.VMEM((rows, local_vars), jnp.bfloat16),
            pltpu.VMEM((ntile, nvar, HOST, tile), jnp.bfloat16),
            pltpu.VMEM((ntile, nvar - 1, HOST, tile), jnp.bfloat16),
            pltpu.SemaphoreType.DMA((ntile, nvar - 1)),
            pltpu.SemaphoreType.DMA((ntile, nvar - 1)),
        ],
        compiler_params=pltpu.CompilerParams(collective_id=2, has_side_effects=True),
        name="lead_exchange",
    )(listed, genotypes)
    return found.reshape(rows, samples)


def places(nx, nz):
    me = lax.axis_index("samp")
    x, z = lax.rem(me, nx), lax.div(me, nx)
    xpeers = [z * nx + lax.rem(x + d, nx) for d in range(1, nx)]
    zpeers = [lax.rem(z + d, nz) * nx + x for d in range(1, nz)]
    return x, z, xpeers, zpeers


def reduce_kernel(
    region_ref,
    slot_ref,
    incoming_ref,
    side_ref,
    geno_ref,
    cross_out,
    small_out,
    gram_out,
    lead,
    weighted,
    cols_buf,
    cross_own,
    small_own,
    gram_own,
    x_cross,
    x_small,
    x_gram,
    mid_cross,
    mid_small,
    mid_gram,
    z_cross,
    z_small,
    z_gram,
    fetched,
    sent_x,
    got_x,
    sent_z,
    got_z,
):
    nx, nz = cross_own.shape[:2]
    nregion, rows, samples = weighted.shape
    nlead = lead.shape[0] // nregion
    chunk_cols = cols_buf.shape[2]
    per_chunk = chunk_cols // VB
    last = nx * nlead
    x, z, xpeers, zpeers = places(nx, nz)
    greet("samp", xpeers + zpeers)

    def turn_of(step):
        turn = lax.rem(step + nz // 2, nz)
        return turn, lax.rem(z + turn, nz)

    def fetch(step):
        chunk = turn_of(step)[1]
        start = pl.multiple_of(chunk * chunk_cols, VB)
        slot = lax.rem(step, 2)
        return pltpu.make_async_copy(
            geno_ref.at[:, pl.ds(start, chunk_cols)], cols_buf.at[slot], fetched.at[slot]
        )

    def remote(source, target, sent, got, peer):
        return pltpu.make_async_remote_copy(
            src_ref=source,
            dst_ref=target,
            send_sem=sent,
            recv_sem=got,
            device_id={"samp": peer},
            device_id_type=pl.DeviceIdType.MESH,
        )

    def x_copies(i, turn):
        trait = lax.rem(x + i + 1, nx)
        return [
            remote(
                cross_own.at[trait, turn],
                x_cross.at[i, turn],
                sent_x.at[0, i, turn],
                got_x.at[0, i, turn],
                xpeers[i],
            ),
            remote(
                small_own.at[trait, turn],
                x_small.at[i, turn],
                sent_x.at[1, i, turn],
                got_x.at[1, i, turn],
                xpeers[i],
            ),
        ]

    def x_gram_copy(i):
        trait = lax.rem(x + i + 1, nx)
        return remote(
            gram_own.at[trait], x_gram.at[i], sent_x.at[0, i, nz], got_x.at[0, i, nz], xpeers[i]
        )

    def z_copies(turn):
        peer = lax.rem(z + turn, nz) * nx + x
        return [
            remote(
                mid_cross.at[turn], z_cross.at[turn], sent_z.at[0, turn], got_z.at[0, turn], peer
            ),
            remote(
                mid_small.at[turn], z_small.at[turn], sent_z.at[1, turn], got_z.at[1, turn], peer
            ),
        ]

    def z_gram_copy(d):
        return remote(
            mid_gram, z_gram.at[d], sent_z.at[2, d], got_z.at[2, d], zpeers[d - 1]
        )

    fetch(0).start()
    slots = incoming_ref.shape[0]
    pick = (
        lax.broadcasted_iota(jnp.int32, (nregion * nlead, slots), 1) == slot_ref[...]
    ).astype(jnp.float32).astype(jnp.bfloat16)
    lead[...] = lax.dot_general(
        pick, incoming_ref[...], NN, preferred_element_type=jnp.float32
    ).astype(jnp.bfloat16)
    for region in range(nregion):
        cols = lead[region * nlead : (region + 1) * nlead, :].astype(jnp.float32)
        for trait in range(nx):
            scale = side_ref[EXTRA + trait : EXTRA + trait + 1, :].astype(jnp.float32)
            weighted[region, trait * nlead : (trait + 1) * nlead, :] = (cols * scale).astype(
                jnp.bfloat16
            )
        weighted[region, last:, :] = side_ref[:EXTRA, :]
        gram = lax.dot_general(
            weighted[region],
            lead[region * nlead : (region + 1) * nlead, :],
            NT,
            preferred_element_type=jnp.float32,
        )
        there = slice(region * nlead, (region + 1) * nlead)
        for trait in range(nx):
            gram_own[trait, :nlead, there] = gram[trait * nlead : (trait + 1) * nlead, :]
            gram_own[trait, nlead : nlead + 1, there] = gram[last + trait : last + trait + 1, :]
            gram_own[trait, nlead + 1 :, there] = jnp.zeros((7, nlead), jnp.float32)
    small_own[...] = jnp.zeros_like(small_own)
    hear(xpeers + zpeers)
    for i in range(nx - 1):
        x_gram_copy(i).start()

    def multiply(step, carry):
        turn, chunk = turn_of(step)
        slot = lax.rem(step, 2)
        fetch(step).wait()

        @pl.when(step < nz - 1)
        def _():
            fetch(step + 1).start()

        for block in range(per_chunk):
            here = slice(block * VB, (block + 1) * VB)
            region = region_ref[chunk * per_chunk + block]
            cols = cols_buf[slot, :, here]
            acc = lax.dot_general(weighted[region], cols, NN, preferred_element_type=jnp.float32)
            square = cols.astype(jnp.float32)
            square = (square * square).astype(jnp.bfloat16)
            diag = lax.dot_general(
                side_ref[EXTRA:, :], square, NN, preferred_element_type=jnp.float32
            )
            other = per_chunk + block
            for trait in range(nx):
                cross_own[trait, turn, :, here] = acc[
                    trait * nlead : (trait + 1) * nlead, :
                ].astype(jnp.bfloat16)
                small_own[trait, turn, block : block + 1, :] = acc[
                    last + trait : last + trait + 1, :
                ]
                small_own[trait, turn, other : other + 1, :] = diag[trait : trait + 1, :]
        for i in range(nx - 1):
            for copy in x_copies(i, turn):
                copy.start()
        return carry

    lax.fori_loop(0, nz, multiply, 0)
    gram = gram_own[x]
    for i in range(nx - 1):
        x_gram_copy(i).wait_recv()
        gram = gram + x_gram[i]
    mid_gram[...] = gram
    for d in range(1, nz):
        z_gram_copy(d).start()

    def combine(step, carry):
        turn = turn_of(step)[0]
        cross = cross_own[x, turn].astype(jnp.float32)
        small = small_own[x, turn]
        for i in range(nx - 1):
            for copy in x_copies(i, turn):
                copy.wait_recv()
            cross = cross + x_cross[i, turn].astype(jnp.float32)
            small = small + x_small[i, turn]
        mid_small[turn] = small

        @pl.when(turn > 0)
        def _():
            mid_cross[turn] = cross.astype(jnp.bfloat16)
            for copy in z_copies(turn):
                copy.start()

        @pl.when(turn == 0)
        def _():
            cross_out[...] = cross

        return carry

    lax.fori_loop(0, nz, combine, 0)
    gram = mid_gram[...]
    small = mid_small[0]
    cross = cross_out[...]
    for d in range(1, nz):
        z_gram_copy(d).wait_recv()
        for copy in z_copies(d):
            copy.wait_recv()
        gram = gram + z_gram[d]
        small = small + z_small[d]
        cross = cross + z_cross[d].astype(jnp.float32)
    gram_out[...] = gram
    small_out[...] = small
    cross_out[...] = cross
    for i in range(nx - 1):
        x_gram_copy(i).wait_send()
        for turn in range(nz):
            for copy in x_copies(i, turn):
                copy.wait_send()
    for d in range(1, nz):
        z_gram_copy(d).wait_send()
        for copy in z_copies(d):
            copy.wait_send()


def cross_products(regions, slot, incoming, side, genotypes, nx, nregion, nz):
    samples, local_vars = genotypes.shape
    nlead = slot.shape[0] // nregion
    chunk = local_vars // nz
    rows = nx * nlead + EXTRA
    vmem = pl.BlockSpec(memory_space=pltpu.VMEM)
    cross = lambda *lead: pltpu.VMEM(lead + (nlead, chunk), jnp.bfloat16)
    small = lambda *lead: pltpu.VMEM(lead + (8, VB), jnp.float32)
    gram = lambda *lead: pltpu.VMEM(lead + (nlead + 8, nregion * nlead), jnp.float32)
    return pl.pallas_call(
        reduce_kernel,
        in_specs=[
            pl.BlockSpec(memory_space=pltpu.SMEM),
            vmem,
            vmem,
            vmem,
            pl.BlockSpec(memory_space=pl.ANY),
        ],
        out_specs=[vmem] * 3,
        out_shape=[
            jax.ShapeDtypeStruct((nlead, chunk), jnp.float32),
            jax.ShapeDtypeStruct((8, VB), jnp.float32),
            jax.ShapeDtypeStruct((nlead + 8, nregion * nlead), jnp.float32),
        ],
        scratch_shapes=[
            pltpu.VMEM((nregion * nlead, samples), jnp.bfloat16),
            pltpu.VMEM((nregion, rows, samples), jnp.bfloat16),
            pltpu.VMEM((2, samples, chunk), jnp.bfloat16),
            cross(nx, nz),
            small(nx, nz),
            gram(nx),
            cross(nx - 1, nz),
            small(nx - 1, nz),
            gram(nx - 1),
            cross(nz),
            small(nz),
            gram(),
            cross(nz),
            small(nz),
            gram(nz),
            pltpu.SemaphoreType.DMA((2,)),
            pltpu.SemaphoreType.DMA((2, nx - 1, nz + 1)),
            pltpu.SemaphoreType.DMA((2, nx - 1, nz + 1)),
            pltpu.SemaphoreType.DMA((3, nz)),
            pltpu.SemaphoreType.DMA((3, nz)),
        ],
        compiler_params=pltpu.CompilerParams(
            collective_id=0, has_side_effects=True, vmem_limit_bytes=48 * 1024 * 1024
        ),
        name="cross_and_reduce",
    )(regions, slot, incoming, side, genotypes)


def share_kernel(nx, nz, result_ref, scores_ref, variances_ref, lane, whole, sent, got, here_sem):
    x, z, xpeers, zpeers = places(nx, nz)
    meet(xpeers + zpeers)
    own = pltpu.make_async_copy(result_ref, lane.at[z], here_sem.at[0])
    own.start()
    first = []
    for i, peer in enumerate(zpeers):
        copy = pltpu.make_async_remote_copy(
            src_ref=result_ref,
            dst_ref=lane.at[z],
            send_sem=sent.at[i],
            recv_sem=got.at[i],
            device_id={"samp": peer},
            device_id_type=pl.DeviceIdType.MESH,
        )
        copy.start()
        first.append(copy)
    own.wait()
    for copy in first:
        copy.wait_recv()
    mine = pltpu.make_async_copy(lane, whole.at[x], here_sem.at[1])
    mine.start()
    second = []
    for i, peer in enumerate(xpeers):
        copy = pltpu.make_async_remote_copy(
            src_ref=lane,
            dst_ref=whole.at[x],
            send_sem=sent.at[nz - 1 + i],
            recv_sem=got.at[nz - 1 + i],
            device_id={"samp": peer},
            device_id_type=pl.DeviceIdType.MESH,
        )
        copy.start()
        second.append(copy)
    mine.wait()
    for copy in second:
        copy.wait_recv()
    per_chunk = scores_ref.shape[1] // (nz * VB)
    for trait in range(nx):
        for chunk in range(nz):
            tile = whole[trait, chunk]
            for block in range(per_chunk):
                at = (chunk * per_chunk + block) * VB
                scores_ref[trait : trait + 1, at : at + VB] = tile[block : block + 1, :]
                variances_ref[trait : trait + 1, at : at + VB] = tile[
                    per_chunk + block : per_chunk + block + 1, :
                ]
    for copy in first + second:
        copy.wait_send()


def share(result, nx, nz, local_vars):
    vmem = pl.BlockSpec(memory_space=pltpu.VMEM)
    out = jax.ShapeDtypeStruct((nx, local_vars), jnp.float32)
    count = nx + nz - 2
    return pl.pallas_call(
        functools.partial(share_kernel, nx, nz),
        in_specs=[vmem],
        out_specs=[vmem] * 2,
        out_shape=[out, out],
        scratch_shapes=[
            pltpu.VMEM((nz,) + result.shape, jnp.float32),
            pltpu.VMEM((nx, nz) + result.shape, jnp.float32),
            pltpu.SemaphoreType.DMA((count,)),
            pltpu.SemaphoreType.DMA((count,)),
            pltpu.SemaphoreType.DMA((2,)),
        ],
        compiler_params=pltpu.CompilerParams(collective_id=1, has_side_effects=True),
        name="share_results",
    )(result)


def finish_kernel(
    traits, total, region_ref, cross_ref, small_ref, gram_ref, out_ref, inverse, pivots, target
):
    nregion, nlead, _ = inverse.shape
    chunk = cross_ref.shape[1]
    per_chunk = chunk // VB
    first = (lax.axis_index("samp") // traits) * per_chunk
    eye = (
        lax.broadcasted_iota(jnp.int32, (nlead, nlead), 0)
        == lax.broadcasted_iota(jnp.int32, (nlead, nlead), 1)
    )
    unit = eye.astype(jnp.float32)
    below = lax.broadcasted_iota(jnp.int32, (nlead, 1), 0)
    state = [
        jnp.concatenate(
            [gram_ref[:nlead, r * nlead : (r + 1) * nlead], unit], axis=1
        )
        for r in range(nregion)
    ]
    for j in range(nlead - 1):
        for r in range(nregion):
            row = state[r][j : j + 1, :]
            ratio = state[r][:, j : j + 1] / row[:, j : j + 1]
            state[r] = state[r] - jnp.where(below > j, ratio, 0.0) * row
    for r in range(nregion):
        lower = state[r][:, nlead:]
        upper = state[r][:, :nlead]
        inverse[r] = lower
        pivot = 1.0 / jnp.sum(jnp.where(eye, upper, 0.0), axis=1, keepdims=True)
        score = gram_ref[nlead : nlead + 1, r * nlead : (r + 1) * nlead]
        pivots[r] = jnp.broadcast_to(pivot, (nlead, VB))
        target[r] = jnp.broadcast_to(
            jnp.sum(lower * score, axis=1, keepdims=True) * pivot, (nlead, VB)
        )
    out_ref[...] = jnp.zeros_like(out_ref)
    for block in range(per_chunk):
        here = slice(block * VB, (block + 1) * VB)
        region = region_ref[first + block]
        solved = lax.dot_general(
            inverse[region],
            cross_ref[:, here],
            NN,
            preferred_element_type=jnp.float32,
            precision=lax.Precision.HIGHEST,
        )
        fit = jnp.sum(solved * target[region], axis=0, keepdims=True)
        used = jnp.sum(solved * solved * pivots[region], axis=0, keepdims=True)
        other = per_chunk + block
        out_ref[block : block + 1, :] = (small_ref[block : block + 1, :] - fit) / math.sqrt(total)
        out_ref[other : other + 1, :] = (small_ref[other : other + 1, :] - used) / total


def finish(regions, cross, small, gram, traits, nlead, nregion, total):
    vmem = pl.BlockSpec(memory_space=pltpu.VMEM)
    return pl.pallas_call(
        functools.partial(finish_kernel, traits, total),
        in_specs=[
            pl.BlockSpec(memory_space=pltpu.SMEM),
            vmem,
            vmem,
            vmem,
        ],
        out_specs=pl.BlockSpec(memory_space=pltpu.VMEM),
        out_shape=jax.ShapeDtypeStruct(small.shape, jnp.float32),
        scratch_shapes=[
            pltpu.VMEM((nregion, nlead, nlead), jnp.float32),
            pltpu.VMEM((nregion, nlead, VB), jnp.float32),
            pltpu.VMEM((nregion, nlead, VB), jnp.float32),
        ],
        name="conditional_finish",
    )(regions, cross, small, gram)


def body(genotypes, residuals, weights, block_regions, leads):
    samples, local_vars = genotypes.shape
    nvar = lax.axis_size("var")
    nsamp = lax.axis_size("samp")
    myself = lax.axis_index("var")
    nregion = leads.shape[0] // nvar
    nlead = leads.shape[1]
    traits = residuals.shape[1]
    nchunk = nsamp // traits
    slots = nregion * nlead
    total = samples * nsamp
    listed = leads.reshape(nvar, slots)
    incoming = gather(listed, genotypes)
    mine = lax.dynamic_index_in_dim(listed, myself, 0, keepdims=False)
    source = mine // local_vars
    order = jnp.arange(slots, dtype=jnp.int32)
    earlier = (source[:, None] == source[None, :]) & (order[None, :] < order[:, None])
    slot = source[:, None] * HOST + jnp.sum(earlier.astype(jnp.int32), axis=1, keepdims=True)
    pad = jnp.zeros((EXTRA - traits, samples), jnp.bfloat16)
    side = jnp.concatenate([residuals.T, pad, weights.T, pad], axis=0)
    cross, small, gram = cross_products(
        block_regions, slot, incoming, side, genotypes, traits, nregion, nchunk
    )
    result = finish(block_regions, cross, small, gram, traits, nlead, nregion, total)
    scores, variances = share(result, traits, nchunk, local_vars)
    return (scores, variances)


def solution(mesh):
    in_specs = (P("samp", "var"), P("samp", None), P("samp", None), P("var"), P())
    out_specs = (P(None, "var"), P(None, "var"))
    return jax.shard_map(body, mesh=mesh, in_specs=in_specs, out_specs=out_specs, check_vma=False)
```

time: 107 us -> 89 us (0.83)
  waiting for transfers between devices: 14.6 us -> 0 us
  starting transfers between devices: 4.47 us -> 0 us
    all_to_all x1 -> x0, waiting for transfers between devices: 14.6 us -> none  [body(): lax.all_to_all(outgoing, 'var', split_axis=0, concat_axis=0, tiled=True)]
    all_to_all x1 -> x0, starting transfers between devices: 4.47 us -> none  [body(): lax.all_to_all(outgoing, 'var', split_axis=0, concat_axis=0, tiled=True)]
    pallas_call x3 -> x2, Pallas kernels: 58.9 us -> 59.1 us  [the longest x1 38.3 us: cross_products(): pl.pallas_call(reduce_kernel, in_specs=[pl.BlockSpec(memory_space=pltpu.S...]
  transfers between devices with their start and end apart: 1 -> 0, of which waited for: 1 -> 0; matrix products, arithmetic and copies ran while one was open for 1% -> 0% of each run, Pallas kernels for 0% -> 0%
where the time goes in v3:
time: 89 us; the launch traced here: 88.3 us
  Pallas kernels  79.5 us (89%)
  local copies, waits for them, and re-layouts  7.05 us (8%)
  other arithmetic  1 us (1%)
    pallas_call x1, Pallas kernels, cross_products(): pl.pallas_call(reduce_kernel, in_specs=[pl.BlockSpec(memory_space=pltpu.S...  38.3 us
    pallas_call x1, Pallas kernels, gather(): pl.pallas_call(gather_kernel, grid=(ntile,), in_specs=[pl.BlockSpec((nvar...  20.8 us
    pallas_call x1, Pallas kernels, share(): pl.pallas_call(functools.partial(share_kernel, nx, nz), in_specs=[vmem],...  13.3 us
    pallas_call x1, Pallas kernels, finish(): pl.pallas_call(functools.partial(finish_kernel, traits, total), in_specs=...  7.13 us
    unnamed x14, local copies, waits for them, and re-layouts  5.91 us

profile of v3, /device:TPU:32, one launch (start us, length us, event | category | flops | bytes accessed | tf_op | source)
XLA Modules:
  0.0 88.3 jit_solution(12581800359729083588)
XLA Ops:
  0.6 0.0 copy-start.4
  0.6 0.8 reshape.92.listed_ref
  1.4 0.0 copy-start.5
  1.4 0.2 convert_reduce_fusion
  1.6 0.1 copy.16
  1.8 0.1 copy.19
  1.9 0.1 copy.15
  2.0 0.8 pad_maximum_fusion.side_ref
  2.8 0.0 copy-done.5
  2.8 20.8 %lead_exchange.1 = bf16[8,32,2048]{2,1,0:T(8,128)(2,1)} custom-call(s32[8,128]{1,0:T(8,128)} %copy-done.5, bf16[2048,3072]{1,0:T(8,128)(2,1)} %geno_ref.3), custom_call_target="tpu_custom_call" | custom-call | tf_op jit(solution)/shard_map/lead_exchange/pallas_call | solution.py:109
  23.6 0.0 copy-done.4
  23.6 0.0 copy-start
  23.6 1.2 %copy-done = bf16[8,32,2048]{2,1,0:T(8,128)(2,1)S(1)} copy-done((bf16[8,32,2048]{2,1,0:T(8,128)(2,1)S(1)}, bf16[8,32,2048]{2,1,0:T(8,128)(2,1)}, u32[]{:S(2)}) %copy-start) | copy-done | bytes 1048600
  24.8 38.3 %cross_and_reduce.1 = (f32[64,384]{1,0:T(8,128)S(1)}, f32[8,128]{1,0:T(8,128)S(1)}, f32[72,128]{1,0:T(8,128)S(1)}) custom-call(s32[24]{0:T(128)S(1)} %copy-done.4, s32[128,1]{1,0:T(8,128)S(1)} %fusion.1.slot_ref, bf16[256,2048]{1,0:T(8,128)(2,1)S(1)} %bitcast.12, bf16[32,2048]{1,0:T(8,128)(2,1)S(1)} %pad_maximum_fusion.side_ref, bf16[2048,3072]{1,0:T(8,128)(2,1)} %geno_ref.3), custom_call_target="tpu_custom_call" | custom-call | tf_op jit(solution)/shard_map/cross_and_reduce/pallas_call | solution.py:372
  63.2 0.0 copy-start.1
  63.2 0.6 copy-done.1
  63.8 0.0 copy-start.2
  63.8 0.6 copy-done.2
  64.4 0.0 copy-start.3
  64.5 0.6 copy-done.3
  65.0 7.1 %conditional_finish.1.result_ref = f32[8,128]{1,0:T(8,128)} custom-call(s32[24]{0:T(128)} %region_ref.3, f32[64,384]{1,0:T(8,128)} %copy-done.1, f32[8,128]{1,0:T(8,128)} %copy-done.3, f32[72,128]{1,0:T(8,128)} %copy-done.2), custom_call_target="tpu_custom_call" | custom-call | tf_op jit(solution)/shard_map/conditional_finish/pallas_call | solution.py:542
  72.2 13.3 %share_results.1 = (f32[4,3072]{1,0:T(4,128)}, f32[4,3072]{1,0:T(4,128)}) custom-call(f32[8,128]{1,0:T(8,128)} %conditional_finish.1.result_ref), custom_call_target="tpu_custom_call" | custom-call | tf_op jit(solution)/shard_map/share_results/pallas_call | solution.py:471
  85.5 1.4 %copy.22 = f32[4,3072]{1,0:T(4,128)} copy(f32[4,3072]{1,0:T(4,128)} %get-tuple-element.13) | data formatting | bytes 98304
  86.9 1.4 %copy.23 = f32[4,3072]{1,0:T(4,128)} copy(f32[4,3072]{1,0:T(4,128)} %get-tuple-element.14) | data formatting | bytes 98304
  (4 shorter events, 0.1 us)
Async XLA Ops:
  0.6 23.0 %copy-start.4 = (s32[24]{0:T(128)S(1)}, s32[24]{0:T(128)}, u32[]{:S(2)}) copy-start(s32[24]{0:T(128)} %region_ref.3) | copy-start | bytes 292
  1.4 1.4 %copy-start.5 = (s32[8,128]{1,0:T(8,128)}, s32[8,128]{1,0:T(8,128)S(1)}, u32[]{:S(2)}) copy-start(s32[8,128]{1,0:T(8,128)S(1)} %reshape.92.listed_ref) | copy-start | bytes 12292
  23.6 1.2 %copy-start = (bf16[8,32,2048]{2,1,0:T(8,128)(2,1)S(1)}, bf16[8,32,2048]{2,1,0:T(8,128)(2,1)}, u32[]{:S(2)}) copy-start(bf16[8,32,2048]{2,1,0:T(8,128)(2,1)} %lead_exchange.1) | copy-start | bytes 3145732
  63.2 0.6 copy-start.1
  63.8 0.6 copy-start.2
  64.4 0.6 copy-start.3

commit v4 on v3

--- a/solution.py
+++ b/solution.py
@@ -25,11 +25,6 @@
 
 def hear(peers):
     pl.semaphore_wait(pltpu.get_barrier_semaphore(), len(peers))
-
-
-def meet(peers):
-    greet("samp", peers)
-    hear(peers)
 
 
 def gather_kernel(listed_ref, geno_ref, out_ref, onehot, leaving, landed, sent, got):
@@ -137,14 +132,14 @@
 
 
 def reduce_kernel(
+    total,
     region_ref,
     slot_ref,
     incoming_ref,
     side_ref,
     geno_ref,
-    cross_out,
-    small_out,
-    gram_out,
+    scores_ref,
+    variances_ref,
     lead,
     weighted,
     cols_buf,
@@ -160,11 +155,20 @@
     z_cross,
     z_small,
     z_gram,
+    cross_sum,
+    inverse,
+    pivots,
+    target,
+    result,
+    lane,
+    whole,
     fetched,
     sent_x,
     got_x,
     sent_z,
     got_z,
+    sent_r,
+    got_r,
 ):
     nx, nz = cross_own.shape[:2]
     nregion, rows, samples = weighted.shape
@@ -278,6 +282,16 @@
         @pl.when(step < nz - 1)
         def _():
             fetch(step + 1).start()
+
+        @pl.when(step == nz // 2)
+        def _():
+            gram = gram_own[x]
+            for i in range(nx - 1):
+                x_gram_copy(i).wait_recv()
+                gram = gram + x_gram[i]
+            mid_gram[...] = gram
+            for d in range(1, nz):
+                z_gram_copy(d).start()
 
         for block in range(per_chunk):
             here = slice(block * VB, (block + 1) * VB)
@@ -304,15 +318,33 @@
         return carry
 
     lax.fori_loop(0, nz, multiply, 0)
-    gram = gram_own[x]
-    for i in range(nx - 1):
-        x_gram_copy(i).wait_recv()
-        gram = gram + x_gram[i]
-    mid_gram[...] = gram
+    gram = mid_gram[...]
     for d in range(1, nz):
-        z_gram_copy(d).start()
-
-    def combine(step, carry):
+        z_gram_copy(d).wait_recv()
+        gram = gram + z_gram[d]
+    down = lax.broadcasted_iota(jnp.int32, (nlead, nlead), 0)
+    across = lax.broadcasted_iota(jnp.int32, (nlead, nlead), 1)
+    eye = down == across
+    tall = lax.broadcasted_iota(jnp.int32, (nlead, 2 * nlead), 0)
+    wide = lax.broadcasted_iota(jnp.int32, (nlead, 2 * nlead), 1)
+    below = lax.broadcasted_iota(jnp.int32, (nlead, 1), 0)
+    state = tuple(
+        jnp.concatenate(
+            [gram[:nlead, r * nlead : (r + 1) * nlead], eye.astype(jnp.float32)], axis=1
+        )
+        for r in range(nregion)
+    )
+    lead_score = gram[nlead : nlead + 1, :]
+
+    def eliminate(j, matrix):
+        row = jnp.sum(jnp.where(tall == j, matrix, 0.0), axis=0, keepdims=True)
+        col = jnp.sum(jnp.where(wide == j, matrix, 0.0), axis=1, keepdims=True)
+        pivot = jnp.sum(jnp.where(below == j, col, 0.0), axis=0, keepdims=True)
+        return matrix - jnp.where(below > j, col / pivot, 0.0) * row
+
+    def combine(step, state):
+        for part in range(nlead // nz):
+            state = tuple(eliminate(step * (nlead // nz) + part, matrix) for matrix in state)
         turn = turn_of(step)[0]
         cross = cross_own[x, turn].astype(jnp.float32)
         small = small_own[x, turn]
@@ -331,24 +363,72 @@
 
         @pl.when(turn == 0)
         def _():
-            cross_out[...] = cross
-
-        return carry
-
-    lax.fori_loop(0, nz, combine, 0)
-    gram = mid_gram[...]
+            cross_sum[...] = cross
+
+        return state
+
+    state = lax.fori_loop(0, nz, combine, state)
+    for r in range(nregion):
+        lower = state[r][:, nlead:]
+        pivot = 1.0 / jnp.sum(jnp.where(eye, state[r][:, :nlead], 0.0), axis=1, keepdims=True)
+        score = lead_score[:, r * nlead : (r + 1) * nlead]
+        inverse[r] = lower
+        pivots[r] = jnp.broadcast_to(pivot, (nlead, VB))
+        target[r] = jnp.broadcast_to(
+            jnp.sum(lower * score, axis=1, keepdims=True) * pivot, (nlead, VB)
+        )
     small = mid_small[0]
-    cross = cross_out[...]
+    cross = cross_sum[...]
     for d in range(1, nz):
-        z_gram_copy(d).wait_recv()
         for copy in z_copies(d):
             copy.wait_recv()
-        gram = gram + z_gram[d]
         small = small + z_small[d]
         cross = cross + z_cross[d].astype(jnp.float32)
-    gram_out[...] = gram
-    small_out[...] = small
-    cross_out[...] = cross
+    result[...] = jnp.zeros_like(result)
+    for block in range(per_chunk):
+        region = region_ref[z * per_chunk + block]
+        other = per_chunk + block
+        solved = lax.dot_general(
+            inverse[region],
+            cross[:, block * VB : (block + 1) * VB],
+            NN,
+            preferred_element_type=jnp.float32,
+            precision=lax.Precision.HIGHEST,
+        )
+        fit = jnp.sum(solved * target[region], axis=0, keepdims=True)
+        used = jnp.sum(solved * solved * pivots[region], axis=0, keepdims=True)
+        result[block : block + 1, :] = (small[block : block + 1, :] - fit) / math.sqrt(total)
+        result[other : other + 1, :] = (small[other : other + 1, :] - used) / total
+
+    first = [
+        remote(result, lane.at[z], sent_r.at[i], got_r.at[i], peer)
+        for i, peer in enumerate(zpeers)
+    ]
+    for copy in first:
+        copy.start()
+    for d in range(1, nz):
+        first[d - 1].wait_recv()
+        whole[x, lax.rem(z + nz - d, nz)] = lane[lax.rem(z + nz - d, nz)]
+    whole[x, z] = result[...]
+    second = [
+        remote(whole.at[x], whole.at[x], sent_r.at[nz - 1 + i], got_r.at[nz - 1 + i], peer)
+        for i, peer in enumerate(xpeers)
+    ]
+    for copy in second:
+        copy.start()
+    for copy in second:
+        copy.wait_recv()
+    for trait in range(nx):
+        for chunk in range(nz):
+            tile = whole[trait, chunk]
+            for block in range(per_chunk):
+                at = (chunk * per_chunk + block) * VB
+                scores_ref[trait : trait + 1, at : at + VB] = tile[block : block + 1, :]
+                variances_ref[trait : trait + 1, at : at + VB] = tile[
+                    per_chunk + block : per_chunk + block + 1, :
+                ]
+    for copy in first + second:
+        copy.wait_send()
     for i in range(nx - 1):
         x_gram_copy(i).wait_send()
         for turn in range(nz):
@@ -360,7 +440,7 @@
             copy.wait_send()
 
 
-def cross_products(regions, slot, incoming, side, genotypes, nx, nregion, nz):
+def conditional(regions, slot, incoming, side, genotypes, nx, nregion, nz, total):
     samples, local_vars = genotypes.shape
     nlead = slot.shape[0] // nregion
     chunk = local_vars // nz
@@ -370,7 +450,7 @@
     small = lambda *lead: pltpu.VMEM(lead + (8, VB), jnp.float32)
     gram = lambda *lead: pltpu.VMEM(lead + (nlead + 8, nregion * nlead), jnp.float32)
     return pl.pallas_call(
-        reduce_kernel,
+        functools.partial(reduce_kernel, total),
         in_specs=[
             pl.BlockSpec(memory_space=pltpu.SMEM),
             vmem,
@@ -378,12 +458,8 @@
             vmem,
             pl.BlockSpec(memory_space=pl.ANY),
         ],
-        out_specs=[vmem] * 3,
-        out_shape=[
-            jax.ShapeDtypeStruct((nlead, chunk), jnp.float32),
-            jax.ShapeDtypeStruct((8, VB), jnp.float32),
-            jax.ShapeDtypeStruct((nlead + 8, nregion * nlead), jnp.float32),
-        ],
+        out_specs=[vmem] * 2,
+        out_shape=[jax.ShapeDtypeStruct((nx, local_vars), jnp.float32)] * 2,
         scratch_shapes=[
             pltpu.VMEM((nregion * nlead, samples), jnp.bfloat16),
             pltpu.VMEM((nregion, rows, samples), jnp.bfloat16),
@@ -400,162 +476,26 @@
             cross(nz),
             small(nz),
             gram(nz),
+            pltpu.VMEM((nlead, chunk), jnp.float32),
+            pltpu.VMEM((nregion, nlead, nlead), jnp.float32),
+            pltpu.VMEM((nregion, nlead, VB), jnp.float32),
+            pltpu.VMEM((nregion, nlead, VB), jnp.float32),
+            small(),
+            small(nz),
+            small(nx, nz),
             pltpu.SemaphoreType.DMA((2,)),
             pltpu.SemaphoreType.DMA((2, nx - 1, nz + 1)),
             pltpu.SemaphoreType.DMA((2, nx - 1, nz + 1)),
             pltpu.SemaphoreType.DMA((3, nz)),
             pltpu.SemaphoreType.DMA((3, nz)),
+            pltpu.SemaphoreType.DMA((nx + nz - 2,)),
+            pltpu.SemaphoreType.DMA((nx + nz - 2,)),
         ],
         compiler_params=pltpu.CompilerParams(
             collective_id=0, has_side_effects=True, vmem_limit_bytes=48 * 1024 * 1024
         ),
-        name="cross_and_reduce",
+        name="conditional_scores",
     )(regions, slot, incoming, side, genotypes)
-
-
-def share_kernel(nx, nz, result_ref, scores_ref, variances_ref, lane, whole, sent, got, here_sem):
-    x, z, xpeers, zpeers = places(nx, nz)
-    meet(xpeers + zpeers)
-    own = pltpu.make_async_copy(result_ref, lane.at[z], here_sem.at[0])
-    own.start()
-    first = []
-    for i, peer in enumerate(zpeers):
-        copy = pltpu.make_async_remote_copy(
-            src_ref=result_ref,
-            dst_ref=lane.at[z],
-            send_sem=sent.at[i],
-            recv_sem=got.at[i],
-            device_id={"samp": peer},
-            device_id_type=pl.DeviceIdType.MESH,
-        )
-        copy.start()
-        first.append(copy)
-    own.wait()
-    for copy in first:
-        copy.wait_recv()
-    mine = pltpu.make_async_copy(lane, whole.at[x], here_sem.at[1])
-    mine.start()
-    second = []
-    for i, peer in enumerate(xpeers):
-        copy = pltpu.make_async_remote_copy(
-            src_ref=lane,
-            dst_ref=whole.at[x],
-            send_sem=sent.at[nz - 1 + i],
-            recv_sem=got.at[nz - 1 + i],
-            device_id={"samp": peer},
-            device_id_type=pl.DeviceIdType.MESH,
-        )
-        copy.start()
-        second.append(copy)
-    mine.wait()
-    for copy in second:
-        copy.wait_recv()
-    per_chunk = scores_ref.shape[1] // (nz * VB)
-    for trait in range(nx):
-        for chunk in range(nz):
-            tile = whole[trait, chunk]
-            for block in range(per_chunk):
-                at = (chunk * per_chunk + block) * VB
-                scores_ref[trait : trait + 1, at : at + VB] = tile[block : block + 1, :]
-                variances_ref[trait : trait + 1, at : at + VB] = tile[
-                    per_chunk + block : per_chunk + block + 1, :
-                ]
-    for copy in first + second:
-        copy.wait_send()
-
-
-def share(result, nx, nz, local_vars):
-    vmem = pl.BlockSpec(memory_space=pltpu.VMEM)
-    out = jax.ShapeDtypeStruct((nx, local_vars), jnp.float32)
-    count = nx + nz - 2
-    return pl.pallas_call(
-        functools.partial(share_kernel, nx, nz),
-        in_specs=[vmem],
-        out_specs=[vmem] * 2,
-        out_shape=[out, out],
-        scratch_shapes=[
-            pltpu.VMEM((nz,) + result.shape, jnp.float32),
-            pltpu.VMEM((nx, nz) + result.shape, jnp.float32),
-            pltpu.SemaphoreType.DMA((count,)),
-            pltpu.SemaphoreType.DMA((count,)),
-            pltpu.SemaphoreType.DMA((2,)),
-        ],
-        compiler_params=pltpu.CompilerParams(collective_id=1, has_side_effects=True),
-        name="share_results",
-    )(result)
-
-
-def finish_kernel(
-    traits, total, region_ref, cross_ref, small_ref, gram_ref, out_ref, inverse, pivots, target
-):
-    nregion, nlead, _ = inverse.shape
-    chunk = cross_ref.shape[1]
-    per_chunk = chunk // VB
-    first = (lax.axis_index("samp") // traits) * per_chunk
-    eye = (
-        lax.broadcasted_iota(jnp.int32, (nlead, nlead), 0)
-        == lax.broadcasted_iota(jnp.int32, (nlead, nlead), 1)
-    )
-    unit = eye.astype(jnp.float32)
-    below = lax.broadcasted_iota(jnp.int32, (nlead, 1), 0)
-    state = [
-        jnp.concatenate(
-            [gram_ref[:nlead, r * nlead : (r + 1) * nlead], unit], axis=1
-        )
-        for r in range(nregion)
-    ]
-    for j in range(nlead - 1):
-        for r in range(nregion):
-            row = state[r][j : j + 1, :]
-            ratio = state[r][:, j : j + 1] / row[:, j : j + 1]
-            state[r] = state[r] - jnp.where(below > j, ratio, 0.0) * row
-    for r in range(nregion):
-        lower = state[r][:, nlead:]
-        upper = state[r][:, :nlead]
-        inverse[r] = lower
-        pivot = 1.0 / jnp.sum(jnp.where(eye, upper, 0.0), axis=1, keepdims=True)
-        score = gram_ref[nlead : nlead + 1, r * nlead : (r + 1) * nlead]
-        pivots[r] = jnp.broadcast_to(pivot, (nlead, VB))
-        target[r] = jnp.broadcast_to(
-            jnp.sum(lower * score, axis=1, keepdims=True) * pivot, (nlead, VB)
-        )
-    out_ref[...] = jnp.zeros_like(out_ref)
-    for block in range(per_chunk):
-        here = slice(block * VB, (block + 1) * VB)
-        region = region_ref[first + block]
-        solved = lax.dot_general(
-            inverse[region],
-            cross_ref[:, here],
-            NN,
-            preferred_element_type=jnp.float32,
-            precision=lax.Precision.HIGHEST,
-        )
-        fit = jnp.sum(solved * target[region], axis=0, keepdims=True)
-        used = jnp.sum(solved * solved * pivots[region], axis=0, keepdims=True)
-        other = per_chunk + block
-        out_ref[block : block + 1, :] = (small_ref[block : block + 1, :] - fit) / math.sqrt(total)
-        out_ref[other : other + 1, :] = (small_ref[other : other + 1, :] - used) / total
-
-
-def finish(regions, cross, small, gram, traits, nlead, nregion, total):
-    vmem = pl.BlockSpec(memory_space=pltpu.VMEM)
-    return pl.pallas_call(
-        functools.partial(finish_kernel, traits, total),
-        in_specs=[
-            pl.BlockSpec(memory_space=pltpu.SMEM),
-            vmem,
-            vmem,
-            vmem,
-        ],
-        out_specs=pl.BlockSpec(memory_space=pltpu.VMEM),
-        out_shape=jax.ShapeDtypeStruct(small.shape, jnp.float32),
-        scratch_shapes=[
-            pltpu.VMEM((nregion, nlead, nlead), jnp.float32),
-            pltpu.VMEM((nregion, nlead, VB), jnp.float32),
-            pltpu.VMEM((nregion, nlead, VB), jnp.float32),
-        ],
-        name="conditional_finish",
-    )(regions, cross, small, gram)
 
 
 def body(genotypes, residuals, weights, block_regions, leads):
@@ -578,11 +518,9 @@
     slot = source[:, None] * HOST + jnp.sum(earlier.astype(jnp.int32), axis=1, keepdims=True)
     pad = jnp.zeros((EXTRA - traits, samples), jnp.bfloat16)
     side = jnp.concatenate([residuals.T, pad, weights.T, pad], axis=0)
-    cross, small, gram = cross_products(
-        block_regions, slot, incoming, side, genotypes, traits, nregion, nchunk
+    scores, variances = conditional(
+        block_regions, slot, incoming, side, genotypes, traits, nregion, nchunk, total
     )
-    result = finish(block_regions, cross, small, gram, traits, nlead, nregion, total)
-    scores, variances = share(result, traits, nchunk, local_vars)
     return (scores, variances)
 
 

time: 89 us -> 75.4 us (0.85)
  Pallas kernels: 79.5 us -> 69.5 us
  local copies, waits for them, and re-layouts: 7.05 us -> 3.61 us
    pallas_call x3 -> x1, Pallas kernels: 58.8 us -> 48.7 us  [conditional(): pl.pallas_call(functools.partial(reduce_kernel, total), in_specs=[pl.Bloc...]
    unnamed x14 -> x8, local copies, waits for them, and re-layouts: 5.91 us -> 2.47 us
where the time goes in v4:
time: 75.4 us; the launch traced here: 74.9 us
  Pallas kernels  69.5 us (92%)
  local copies, waits for them, and re-layouts  3.61 us (5%)
  other arithmetic  1 us (1%)
    pallas_call x1, Pallas kernels, conditional(): pl.pallas_call(functools.partial(reduce_kernel, total), in_specs=[pl.Bloc...  48.7 us
    pallas_call x1, Pallas kernels, gather(): pl.pallas_call(gather_kernel, grid=(ntile,), in_specs=[pl.BlockSpec((nvar...  20.8 us
    unnamed x8, local copies, waits for them, and re-layouts  2.47 us

profile of v4, /device:TPU:32, one launch (start us, length us, event | category | flops | bytes accessed | tf_op | source)
XLA Modules:
  0.0 74.9 jit_solution(12920750835098064687)
XLA Ops:
  0.6 0.0 copy-start.1
  0.6 0.8 %reshape.92.listed_ref = s32[8,128]{1,0:T(8,128)S(1)} reshape(s32[16,64]{1,0:T(8,128)} %param.9) | data formatting | bytes 8192 | tf_op jit(solution)/shard_map/reshape | solution.py:512
  1.4 0.0 copy-start.2
  1.4 0.2 convert_reduce_fusion
  1.6 0.1 copy.16
  1.8 0.1 copy.19
  1.9 0.1 copy.15
  2.0 0.8 %pad_maximum_fusion.side_ref = bf16[32,2048]{1,0:T(8,128)(2,1)S(1)} fusion(bf16[12,2048]{1,0:T(8,128)(2,1)S(1)} %broadcast_in_dim.2, bf16[4,2048]{1,0:T(4,128)(2,1)} %bitcast.13, bf16[4,2048]{1,0:T(4,128)(2,1)} %bitcast.14), kind=kLoop, calls=%fused_computation | loop fusion | flops 524288 | bytes 212992 | tf_op jit(solution)/shard_map/concatenate | solution.py:520
  2.8 0.0 copy-done.2
  2.8 20.8 %lead_exchange.1 = bf16[8,32,2048]{2,1,0:T(8,128)(2,1)} custom-call(s32[8,128]{1,0:T(8,128)} %copy-done.2, bf16[2048,3072]{1,0:T(8,128)(2,1)} %geno_ref.3), custom_call_target="tpu_custom_call" | custom-call | tf_op jit(solution)/shard_map/lead_exchange/pallas_call | solution.py:104
  23.6 0.0 copy-done.1
  23.6 0.0 copy-start
  23.6 1.2 %copy-done = bf16[8,32,2048]{2,1,0:T(8,128)(2,1)S(1)} copy-done((bf16[8,32,2048]{2,1,0:T(8,128)(2,1)S(1)}, bf16[8,32,2048]{2,1,0:T(8,128)(2,1)}, u32[]{:S(2)}) %copy-start) | copy-done | bytes 1048600
  24.9 48.7 %conditional_scores.1 = (f32[4,3072]{1,0:T(4,128)S(1)}, f32[4,3072]{1,0:T(4,128)S(1)}) custom-call(s32[24]{0:T(128)S(1)} %copy-done.1, s32[128,1]{1,0:T(8,128)S(1)} %fusion.1.slot_ref, bf16[256,2048]{1,0:T(8,128)(2,1)S(1)} %bitcast.12, bf16[32,2048]{1,0:T(8,128)(2,1)S(1)} %pad_maximum_fusion.side_ref, bf16[2048,3072]{1,0:T(8,128)(2,1)} %geno_ref.3), custom_call_target="tpu_custom_call" | custom-call | tf_op jit(solution)/shard_map/conditional_scores/pallas_call | solution.py:452
  73.6 0.6 copy.22
  74.2 0.6 copy.23
  (4 shorter events, 0.1 us)
Async XLA Ops:
  0.6 23.0 %copy-start.1 = (s32[24]{0:T(128)S(1)}, s32[24]{0:T(128)}, u32[]{:S(2)}) copy-start(s32[24]{0:T(128)} %region_ref.1) | copy-start | bytes 292
  1.4 1.4 %copy-start.2 = (s32[8,128]{1,0:T(8,128)}, s32[8,128]{1,0:T(8,128)S(1)}, u32[]{:S(2)}) copy-start(s32[8,128]{1,0:T(8,128)S(1)} %reshape.92.listed_ref) | copy-start | bytes 12292
  23.6 1.2 %copy-start = (bf16[8,32,2048]{2,1,0:T(8,128)(2,1)S(1)}, bf16[8,32,2048]{2,1,0:T(8,128)(2,1)}, u32[]{:S(2)}) copy-start(bf16[8,32,2048]{2,1,0:T(8,128)(2,1)} %lead_exchange.1) | copy-start | bytes 3145732

commit v5 on v4

--- a/solution.py
+++ b/solution.py
@@ -13,6 +13,7 @@
 NT = (((1,), (1,)), ((), ()))
 NN = (((1,), (0,)), ((), ()))
 EXTRA = 16
+DIRECT, MERGED, RELAY = range(3)
 
 
 def greet(axis, peers):
@@ -147,6 +148,7 @@
     small_own,
     gram_own,
     x_cross,
+    x_merge,
     x_small,
     x_gram,
     mid_cross,
@@ -201,24 +203,39 @@
             device_id_type=pl.DeviceIdType.MESH,
         )
 
-    def x_copies(i, turn):
-        trait = lax.rem(x + i + 1, nx)
-        return [
-            remote(
-                cross_own.at[trait, turn],
-                x_cross.at[i, turn],
-                sent_x.at[0, i, turn],
-                got_x.at[0, i, turn],
-                xpeers[i],
-            ),
-            remote(
-                small_own.at[trait, turn],
-                x_small.at[i, turn],
-                sent_x.at[1, i, turn],
-                got_x.at[1, i, turn],
-                xpeers[i],
-            ),
-        ]
+    def x_small_copy(i, turn):
+        return remote(
+            small_own.at[lax.rem(x + i + 1, nx), turn],
+            x_small.at[i, turn],
+            sent_x.at[1, i, turn],
+            got_x.at[1, i, turn],
+            xpeers[i],
+        )
+
+    def x_copy(kind, turn):
+        ahead = 1 + (nx - 2) * lax.rem(turn, 2)
+        front, back, far = (lax.rem(x + d, nx) for d in (ahead, nx - ahead, 2))
+        source, peer = (
+            (cross_own.at[back, turn], back),
+            (x_merge.at[turn], front),
+            (cross_own.at[far, turn], front),
+        )[kind]
+        return remote(
+            source,
+            x_cross.at[kind, turn],
+            sent_x.at[0, kind, turn],
+            got_x.at[0, kind, turn],
+            z * nx + peer,
+        )
+
+    def pass_on(step):
+        turn = turn_of(step)[0]
+        front = lax.rem(x + 1 + (nx - 2) * lax.rem(turn, 2), nx)
+        x_copy(RELAY, turn).wait_recv()
+        x_merge[turn] = (
+            cross_own[front, turn].astype(jnp.float32) + x_cross[2, turn].astype(jnp.float32)
+        ).astype(jnp.bfloat16)
+        x_copy(MERGED, turn).start()
 
     def x_gram_copy(i):
         trait = lax.rem(x + i + 1, nx)
@@ -312,12 +329,19 @@
                     last + trait : last + trait + 1, :
                 ]
                 small_own[trait, turn, other : other + 1, :] = diag[trait : trait + 1, :]
+        x_copy(RELAY, turn).start()
+        x_copy(DIRECT, turn).start()
         for i in range(nx - 1):
-            for copy in x_copies(i, turn):
-                copy.start()
+            x_small_copy(i, turn).start()
+
+        @pl.when(step > 0)
+        def _():
+            pass_on(step - 1)
+
         return carry
 
     lax.fori_loop(0, nz, multiply, 0)
+    pass_on(nz - 1)
     gram = mid_gram[...]
     for d in range(1, nz):
         z_gram_copy(d).wait_recv()
@@ -348,10 +372,11 @@
         turn = turn_of(step)[0]
         cross = cross_own[x, turn].astype(jnp.float32)
         small = small_own[x, turn]
+        for kind in (DIRECT, MERGED):
+            x_copy(kind, turn).wait_recv()
+            cross = cross + x_cross[kind, turn].astype(jnp.float32)
         for i in range(nx - 1):
-            for copy in x_copies(i, turn):
-                copy.wait_recv()
-            cross = cross + x_cross[i, turn].astype(jnp.float32)
+            x_small_copy(i, turn).wait_recv()
             small = small + x_small[i, turn]
         mid_small[turn] = small
 
@@ -432,8 +457,10 @@
     for i in range(nx - 1):
         x_gram_copy(i).wait_send()
         for turn in range(nz):
-            for copy in x_copies(i, turn):
-                copy.wait_send()
+            x_small_copy(i, turn).wait_send()
+    for turn in range(nz):
+        for kind in (DIRECT, MERGED, RELAY):
+            x_copy(kind, turn).wait_send()
     for d in range(1, nz):
         z_gram_copy(d).wait_send()
         for copy in z_copies(d):
@@ -468,6 +495,7 @@
             small(nx, nz),
             gram(nx),
             cross(nx - 1, nz),
+            cross(nz),
             small(nx - 1, nz),
             gram(nx - 1),
             cross(nz),

time: 75.4 us -> 80.7 us (1.070)
  Pallas kernels: 69.5 us -> 75 us
    pallas_call x1, Pallas kernels: 48.7 us -> 54.2 us  [conditional(): pl.pallas_call(functools.partial(reduce_kernel, total), in_specs=[pl.Bloc...]
where the time goes in v5:
time: 80.7 us; the launch traced here: 80.3 us
  Pallas kernels  75 us (93%)
  local copies, waits for them, and re-layouts  3.61 us (4%)
  other arithmetic  1 us (1%)
    pallas_call x1, Pallas kernels, conditional(): pl.pallas_call(functools.partial(reduce_kernel, total), in_specs=[pl.Bloc...  54.2 us
    pallas_call x1, Pallas kernels, gather(): pl.pallas_call(gather_kernel, grid=(ntile,), in_specs=[pl.BlockSpec((nvar...  20.8 us
    unnamed x8, local copies, waits for them, and re-layouts  2.47 us

profile of v5, /device:TPU:32, one launch (start us, length us, event | category | flops | bytes accessed | tf_op | source)
XLA Modules:
  0.0 80.3 jit_solution(11223771444117936993)
XLA Ops:
  0.6 0.0 copy-start.1
  0.6 0.8 reshape.92.listed_ref
  1.4 0.0 copy-start.2
  1.4 0.2 convert_reduce_fusion
  1.6 0.1 copy.16
  1.8 0.1 copy.19
  1.9 0.1 copy.15
  2.0 0.8 pad_maximum_fusion.side_ref
  2.8 0.0 copy-done.2
  2.8 20.8 %lead_exchange.1 = bf16[8,32,2048]{2,1,0:T(8,128)(2,1)} custom-call(s32[8,128]{1,0:T(8,128)} %copy-done.2, bf16[2048,3072]{1,0:T(8,128)(2,1)} %geno_ref.3), custom_call_target="tpu_custom_call" | custom-call | tf_op jit(solution)/shard_map/lead_exchange/pallas_call | solution.py:105
  23.6 0.0 copy-done.1
  23.6 0.0 copy-start
  23.6 1.2 %copy-done = bf16[8,32,2048]{2,1,0:T(8,128)(2,1)S(1)} copy-done((bf16[8,32,2048]{2,1,0:T(8,128)(2,1)S(1)}, bf16[8,32,2048]{2,1,0:T(8,128)(2,1)}, u32[]{:S(2)}) %copy-start) | copy-done | bytes 1048600
  24.9 54.2 %conditional_scores.1 = (f32[4,3072]{1,0:T(4,128)S(1)}, f32[4,3072]{1,0:T(4,128)S(1)}) custom-call(s32[24]{0:T(128)S(1)} %copy-done.1, s32[128,1]{1,0:T(8,128)S(1)} %fusion.1.slot_ref, bf16[256,2048]{1,0:T(8,128)(2,1)S(1)} %bitcast.12, bf16[32,2048]{1,0:T(8,128)(2,1)S(1)} %pad_maximum_fusion.side_ref, bf16[2048,3072]{1,0:T(8,128)(2,1)} %geno_ref.3), custom_call_target="tpu_custom_call" | custom-call | tf_op jit(solution)/shard_map/conditional_scores/pallas_call | solution.py:479
  79.1 0.6 copy.22
  79.7 0.6 copy.23
  (4 shorter events, 0.1 us)
Async XLA Ops:
  0.6 23.0 %copy-start.1 = (s32[24]{0:T(128)S(1)}, s32[24]{0:T(128)}, u32[]{:S(2)}) copy-start(s32[24]{0:T(128)} %region_ref.1) | copy-start | bytes 292
  1.4 1.4 %copy-start.2 = (s32[8,128]{1,0:T(8,128)}, s32[8,128]{1,0:T(8,128)S(1)}, u32[]{:S(2)}) copy-start(s32[8,128]{1,0:T(8,128)S(1)} %reshape.92.listed_ref) | copy-start | bytes 12292
  23.6 1.2 %copy-start = (bf16[8,32,2048]{2,1,0:T(8,128)(2,1)S(1)}, bf16[8,32,2048]{2,1,0:T(8,128)(2,1)}, u32[]{:S(2)}) copy-start(bf16[8,32,2048]{2,1,0:T(8,128)(2,1)} %lead_exchange.1) | copy-start | bytes 3145732
